TPU v7x, 32 devices: a whole 2x2x4 slice. The times are simulated.
32 devices in a mesh: row: 8 (over y, x, core), col: 4 (over z).
Axes of the slice: x: 2, y: 2, z: 4, core: 2. Of those that a mesh axis runs over, the one named last changes fastest.
Arguments:
- covariance: float32 [4096, 2, 2048], P('row', None, 'col'), may hold values from 0 to 1.1, as said below
- diag_inverse: float32 [512, 512], replicated, as said below
Outputs:
- panels: float32 [4096, 1024], P('row', 'col')
- trailing: float32 [4096, 2, 2048], P('row', None, 'col')
Inputs may be any that keep to these rules, and one draw needn't show every extreme that they name: `covariance`: K is symmetric and positive definite, its smallest eigenvalue 0.1 or more. `diag_inverse`: the inverse of the lower Cholesky factor of K[0:512, 0:512].
All inputs are finite; a program needn't handle non-finite values.
Results may differ from a plain program's by a relative error of at most 0.0003.
Values sent between devices are 32-bit elements; how exact they have to be, the bound alone decides.
No kernel may reach another device: no remote copies, remote signals or barrier semaphores. Data moves between devices by JAX's collectives and lax.ppermute only.
A program may use at most 128 MiB of HBM per device.

v0:
```python
import functools

import jax
import jax.numpy as jnp
from jax import lax
from jax.experimental import pallas as pl
from jax.experimental.pallas import tpu as pltpu
from jax.sharding import PartitionSpec as P

HIGHEST = lax.Precision.HIGHEST
AXES = ("row", "col")
SUB = 8


def dot(left, right, lhs_dim, rhs_dim):
    return lax.dot_general(
        left,
        right,
        (((lhs_dim,), (rhs_dim,)), ((), ())),
        precision=HIGHEST,
        preferred_element_type=jnp.float32,
    )


def nn(left, right):
    return dot(left, right, 1, 0)


def nt(left, right):
    return dot(left, right, 1, 1)


def tn(left, right):
    return dot(left, right, 0, 0)


def halves(value):
    high = value.astype(jnp.bfloat16)
    return high, (value - high.astype(jnp.float32)).astype(jnp.bfloat16)


def dot3(left, right, lhs_dim, rhs_dim):
    (a, b), (x, y) = halves(left), halves(right)

    def part(u, v):
        return lax.dot_general(
            u, v, (((lhs_dim,), (rhs_dim,)), ((), ())), preferred_element_type=jnp.float32
        )

    return part(a, x) + (part(a, y) + part(b, x))


def factor_block(work, aug):
    size = work.shape[0]
    groups = size // SUB
    rows = lax.broadcasted_iota(jnp.int32, (SUB, size), 0)
    lanes = lax.broadcasted_iota(jnp.int32, (SUB, size), 1)
    for t in range(groups):
        aug[t * SUB : (t + 1) * SUB, :] = jnp.where(lanes == rows + t * SUB, 1.0, 0.0)

    def lane(value, index):
        return jnp.broadcast_to(value[:, index : index + 1], (SUB, size))

    def row(value, index):
        return jnp.broadcast_to(value[index : index + 1, :], (SUB, size))

    for s in range(groups):
        here = slice(s * SUB, (s + 1) * SUB)
        own, own_aug = work[here, :], aug[here, :]
        columns = [lane(own, s * SUB + b) for b in range(SUB)]
        small = [[row(columns[b], a) if a >= b else None for b in range(SUB)] for a in range(SUB)]
        upper = [row(own, i) for i in range(SUB)]
        inverse = [row(own_aug, i) for i in range(SUB)]
        low = [[None] * SUB for _ in range(SUB)]
        scale = []
        for i in range(SUB):
            scale.append(lax.rsqrt(small[i][i]))
            for a in range(i + 1, SUB):
                low[a][i] = small[a][i] * scale[i]
            for b in range(i + 1, SUB):
                for a in range(b, SUB):
                    small[a][b] = small[a][b] - low[a][i] * low[b][i]
            upper[i] = upper[i] * scale[i]
            inverse[i] = inverse[i] * scale[i]
            for b in range(i + 1, SUB):
                upper[b] = upper[b] - upper[i] * low[b][i]
                inverse[b] = inverse[b] - inverse[i] * low[b][i]
        for t in range(s + 1, groups):
            there = slice(t * SUB, (t + 1) * SUB)
            current, current_aug = work[there, :], aug[there, :]
            part = [lane(current, s * SUB + b) for b in range(SUB)]
            for i in range(SUB):
                part[i] = part[i] * scale[i]
                for b in range(i + 1, SUB):
                    part[b] = part[b] - part[i] * low[b][i]
                current = current - part[i] * upper[i]
                current_aug = current_aug - part[i] * inverse[i]
            work[there, :] = current
            aug[there, :] = current_aug
        packed = inverse[0]
        for i in range(1, SUB):
            packed = jnp.where(rows == i, inverse[i], packed)
        aug[here, :] = packed


def masks(shape):
    return lax.broadcasted_iota(jnp.int32, shape, 0), lax.broadcasted_iota(jnp.int32, shape, 1)


def unpack(packed):
    half = packed.shape[1] // 2
    block = packed[:half, :half]
    rows, lanes = masks(block.shape)
    diag = jnp.broadcast_to(packed[half : half + 1, :half], block.shape)
    first = jnp.where(lanes <= rows, block, 0.0)
    second_t = jnp.where(lanes > rows, block, jnp.where(lanes == rows, diag, 0.0))
    return first, packed[:half, half:], second_t


def place():
    return lax.axis_index("row"), lax.axis_index("col")


def fetch(target, semaphore, choices):
    for condition, source in choices:

        @pl.when(condition)
        def _(source=source):
            pltpu.make_async_copy(source, target, semaphore).start()

    return pltpu.make_async_copy(choices[0][1], target, semaphore).wait


def call(kernel, out_shapes, inputs, scratch, vmem_inputs=0, flops=0):
    outs = [jax.ShapeDtypeStruct(shape, jnp.float32) for shape in out_shapes]
    size = sum(4 * x.size for x in inputs) + sum(4 * x.size for x in outs)
    return pl.pallas_call(
        kernel,
        out_shape=outs,
        in_specs=[
            pl.BlockSpec(memory_space=pltpu.VMEM if i < vmem_inputs else pl.ANY)
            for i in range(len(inputs))
        ],
        out_specs=[pl.BlockSpec(memory_space=pltpu.VMEM)] * len(outs),
        scratch_shapes=scratch,
        cost_estimate=pl.CostEstimate(flops=flops, bytes_accessed=size, transcendentals=0),
    )(*inputs)


def vmem(*shape):
    return pltpu.VMEM(shape, jnp.float32)


def copies(count):
    return pltpu.SemaphoreType.DMA((count,))


def split(refs, *counts):
    groups = []
    for count in counts:
        groups.append(refs[:count])
        refs = refs[count:]
    return groups


def extract_kernel(cov_ref, diag_ref, lead_ref, own_ref, low_ref, high_ref, *refs):
    held_refs, dinv, sems = refs[:-2], refs[-2], refs[-1]
    half = low_ref.shape[0]
    cycles = cov_ref.shape[1]
    r, c = place()
    source = (r == 0) & (c == 1)

    @pl.when(source)
    def _():
        pltpu.make_async_copy(diag_ref, dinv, sems.at[0]).start()

    own = cov_ref[:, 0, :]
    own_ref[...] = own
    low_ref[...] = own[:half]
    high_ref[...] = own[half:]
    for t, held_ref in enumerate(held_refs):
        later = cov_ref[:, min(t + 1, cycles - 1), :]
        held_ref[...] = jnp.where(c < 2, later, cov_ref[:, t, :])

    @pl.when(source)
    def _():
        pltpu.make_async_copy(diag_ref, dinv, sems.at[0]).wait()
        lead_ref[...] = nn(dinv[...], own_ref[...])

    @pl.when(jnp.logical_not(source))
    def _():
        lead_ref[...] = own_ref[...]


def factor_kernel(corner_ref, own_ref, out_ref, corner, second, diag, aug, first, last, cross, wide, sems):
    half = first.shape[0]
    part = half // 2
    r, c = place()
    owner = (r == 1) & (c == 1)
    a, b, low, high = slice(0, part), slice(part, half), slice(0, half), slice(half, 2 * half)

    @pl.when(owner)
    def _():
        waits = [
            fetch(corner, sems.at[0], [(owner, corner_ref)]),
            fetch(second, sems.at[1], [(owner, own_ref)]),
        ]
        for wait in waits:
            wait()
        second[...] = second[...] - tn(corner[...], corner[...])
        diag[...] = second[a, a]

        def upper_stage(inverse, base):
            inv = aug[...]
            inverse[a, a] = inv
            inverse[a, b] = jnp.zeros_like(inv)
            rows = slice(base, base + part)
            later = slice(base + part, base + half)
            cross[...] = nn(inv, second[rows, later])
            diag[...] = second[later, later] - tn(cross[...], cross[...])

        def lower_stage(inverse):
            inv = aug[...]
            inverse[b, b] = inv
            inverse[b, a] = -nn(inv, tn(cross[...], inverse[a, a]))

        def step(k, carry):
            factor_block(diag, aug)

            @pl.when(k == 0)
            def _():
                upper_stage(first, 0)

            @pl.when(k == 1)
            def _():
                lower_stage(first)
                wide[...] = nn(first[...], second[low, high])
                second[high, high] = second[high, high] - tn(wide[...], wide[...])
                diag[...] = second[half : half + part, half : half + part]

            @pl.when(k == 2)
            def _():
                upper_stage(last, half)

            @pl.when(k == 3)
            def _():
                lower_stage(last)

            return carry

        lax.fori_loop(0, 4, step, 0)
        inv = last[...]
        rows, lanes = masks(inv.shape)
        out_ref[:half, :half] = jnp.where(lanes <= rows, first[...], inv.T)
        out_ref[:half, half:] = -nn(inv, tn(wide[...], first[...]))
        diagonal = jnp.sum(jnp.where(lanes == rows, inv, 0.0), axis=0, keepdims=True)
        out_ref[half:, :half] = jnp.broadcast_to(diagonal, (SUB, half))
        out_ref[half:, half:] = jnp.zeros((SUB, half), jnp.float32)


def early_kernel(cols, cycles, tiles, *refs):
    hops = cols - 1
    (own, diag, near_held), low, high, mine, other, held, (panel_ref, near_ref), first_t, part, rest = split(
        refs, 3, hops, hops, tiles, tiles, tiles, 2, tiles, tiles, 4
    )
    first, dinv, column, sems = rest
    half = low[0].shape[0]
    r, c = place()
    core = r % 2
    always = c >= 0
    waits = [fetch(dinv, sems.at[0], [(always, diag)])]
    for i, parts in enumerate((low, high)):
        rows = pl.ds(i * half, half)
        choices = [(c == 0, own.at[rows])]
        choices += [(c == b, parts[b - 1]) for b in range(1, cols)]
        waits.append(fetch(first.at[rows], sems.at[1 + i], choices))
    for wait in waits:
        wait()
    panel_ref[...] = nt(first[...], dinv[...])
    for t in range(tiles):
        index = (t + jnp.where(c < 2, 1, 0)) * cols + c

        @pl.when(r >= index)
        def _(t=t):
            waits = [
                fetch(column, sems.at[3], [(core == 0, mine[t]), (core == 1, other[t])]),
                fetch(part[t], sems.at[4], [(always, held[t])]),
            ]
            for wait in waits:
                wait()
            first_t[t][...] = nn(dinv[...], column[...])
            part[t][...] = part[t][...] - nn(panel_ref[...], first_t[t][...])

    @pl.when((c >= 2) & (r == (cycles - 1) * cols + c))
    def _():
        fetch(near_ref, sems.at[4], [(always, near_held)])()
        near_ref[...] = near_ref[...] - nt(panel_ref[...], panel_ref[...])


def middle_kernel(cols, tiles, *refs):
    (even, odd, panel, own, back), low, high, mine, other, first_t, (pair_ref,), schur_t, rest = split(
        refs, 5, cols - 1, cols - 1, tiles, tiles, tiles, 1, tiles, 3
    )
    corner, column, sems = rest
    half = low[0].shape[0]
    r, c = place()
    core = r % 2
    always = c >= 0
    top, bottom = pl.ds(0, 2 * half), pl.ds(2 * half, 2 * half)
    waits = [
        fetch(corner, sems.at[0], [(core == 0, even), (core == 1, odd)]),
        fetch(pair_ref.at[top], sems.at[1], [(always, panel)]),
    ]
    for i, parts in enumerate((low, high)):
        rows = pl.ds(i * half, half)
        choices = [(c == 0, back.at[rows]), (c == 1, own.at[rows])]
        choices += [(c == b, parts[b - 2]) for b in range(2, cols)]
        waits.append(fetch(pair_ref.at[pl.ds((2 + i) * half, half)], sems.at[2 + i], choices))
    for wait in waits:
        wait()

    @pl.when(r == 1)
    def _():
        pair_ref[top, :] = corner[...].T

    pair_ref[bottom, :] = pair_ref[bottom, :] - nn(pair_ref[top, :], corner[...])
    for t in range(tiles):
        index = (t + jnp.where(c < 2, 1, 0)) * cols + c

        @pl.when(r >= index)
        def _(t=t):
            waits = [
                fetch(column, sems.at[4], [(always, first_t[t])]),
                fetch(schur_t[t], sems.at[5], [(core == 1, mine[t]), (core == 0, other[t])]),
            ]
            for wait in waits:
                wait()
            schur_t[t][...] = schur_t[t][...] - tn(corner[...], column[...])


def late_kernel(cols, cycles, tiles, *refs):
    (even, odd, pair, near_pair, held, near_part), first_part, schur_t, outs, rest = split(
        refs, 6, tiles, tiles, 2, 6
    )
    panels_ref, trailing_ref = outs
    packed, stack, other, column, total, sems = rest
    tile = total.shape[0]
    half = tile // 2
    low, high = slice(0, half), slice(half, tile)
    first, second = slice(0, tile), slice(tile, 2 * tile)
    r, c = place()
    core = r % 2
    always = c >= 0
    last = (cycles - 1) * cols + c
    own = (c >= 2) & (r == last)
    near = (c >= 2) & (r == last + 1) & (r // 2 == last // 2)
    waits = [
        fetch(packed, sems.at[0], [(core == 0, even), (core == 1, odd)]),
        fetch(stack, sems.at[1], [(always, pair)]),
    ]
    for wait in waits:
        wait()
    g_first, g_below, g_second_t = unpack(packed[...])

    def solve(target):
        left, right = target[second, low], target[second, high]
        target[second, low] = dot3(left, g_first, 1, 1)
        target[second, high] = dot3(left, g_below, 1, 1) + dot3(right, g_second_t, 1, 0)

    @pl.when(r == 0)
    def _():
        stack[second, :] = jnp.zeros((tile, tile), jnp.float32)

    @pl.when(r > 0)
    def _():
        solve(stack)

    width = panels_ref.shape[1]
    for b in range(cols):

        @pl.when(c == b)
        def _(b=b):
            rows, start = (first, b * width) if 2 * b < cols else (second, b * width - tile)
            panels_ref[...] = stack[rows, start : start + width]

    trailing_ref[...] = jnp.zeros_like(trailing_ref)

    def store(t):
        for shift in (0, 1):
            if t + shift < cycles:

                @pl.when((c < 2) if shift else (c >= 2))
                def _(slot=t + shift):
                    trailing_ref[:, slot, :] = total[...]

    for t in range(tiles):
        index = (t + jnp.where(c < 2, 1, 0)) * cols + c
        wanted = r >= index
        if t + 1 == cycles:
            wanted = wanted & jnp.logical_not(own | near)

        @pl.when(wanted)
        def _(t=t):
            waits = [
                fetch(column, sems.at[2], [(always, schur_t[t])]),
                fetch(total, sems.at[3], [(always, first_part[t])]),
            ]
            for wait in waits:
                wait()
            upper, lower = column[low], column[high]
            column[low] = dot3(g_first, upper, 1, 0)
            column[high] = dot3(g_below, upper, 1, 0) + dot3(g_second_t, lower, 0, 0)
            total[...] = total[...] - dot3(stack[second, :], column[...], 1, 0)
            store(t)

    @pl.when(own)
    def _():
        fetch(total, sems.at[3], [(always, near_part)])()
        other[second, :] = stack[second, :]

    @pl.when(near)
    def _():
        waits = [
            fetch(other, sems.at[2], [(always, near_pair)]),
            fetch(total, sems.at[3], [(always, held)]),
        ]
        for wait in waits:
            wait()
        solve(other)
        total[...] = total[...] - nt(stack[first, :], other[first, :])

    @pl.when(own | near)
    def _():
        total[...] = total[...] - dot3(stack[second, :], other[second, :], 1, 1)
        store(cycles - 1)


def local(covariance, diag_inverse, rows, cols):
    tile = covariance.shape[0]
    cycles = covariance.shape[1]
    half = tile // 2
    chips = rows // 2
    r, c = place()
    chip, core = r // 2, r % 2
    whole = (tile, tile)

    def send(value, pairs):
        flat = [(a * cols + b, x * cols + y) for (a, b), (x, y) in pairs]
        return lax.ppermute(value, AXES, flat)

    bits = []
    while (1 << len(bits)) < chips:
        bits.append(1 << len(bits))

    def column_of(t, column):
        return (t + (1 if column < 2 else 0)) * cols + column

    lead, own, own_low, own_high, *held = call(
        extract_kernel,
        [whole, whole, (half, tile), (half, tile)] + [whole] * cycles,
        [covariance, diag_inverse],
        [vmem(*whole), copies(1)],
        vmem_inputs=1,
    )

    swapped = send(lead, [((0, 1), (1, 1))])

    def along(column, hop):
        source = column - hop
        return [
            ((a, column), (a, column + 1))
            for a in range(rows)
            if (a >= 2 and source in (0, 1))
            or (a == 0 and source == 0 and hop == 0)
            or (a == 1 and source == 1)
        ]

    moved = []
    for part in (own_low, own_high):
        chain = []
        for hop in range(cols - 1):
            pairs = [pair for column in range(cols - 1) for pair in along(column, hop)]
            part = send(part, pairs)
            chain.append(part)
        moved.append(chain)
    back = send(lead, [((a, 1), (a, 0)) for a in range(rows) if a == 0 or a >= min(cols, rows - 1)])

    def spread(value, wanted, cores):
        current = value
        for step in range(len(bits)):
            pairs = []
            arrived = False
            for k in cores:
                order = bits if k == 0 else bits[::-1]
                used, bit, later = sum(order[:step]), order[step], sum(order[step + 1 :])
                arrived = jnp.where(core == k, (chip & bit) != 0, arrived)
                for column in range(cols):
                    for q in range(chips):
                        target = q | bit
                        if q & ~used or target >= chips:
                            continue
                        reach = {target | extra for extra in range(chips) if not extra & ~later}
                        if reach & wanted(column):
                            pairs.append(((2 * q + k, column), (2 * target + k, column)))
            if pairs:
                current = jnp.where(arrived, send(current, pairs), current)
        return current

    def trade(value, wanted, ways=(0, 1)):
        pairs = []
        for column in range(cols):
            for q in wanted(column):
                pairs += [((2 * q + k, column), (2 * q + 1 - k, column)) for k in ways]
        return send(value, pairs)

    mine, other = [], []
    for t in range(cycles):

        def wanted(column, t=t):
            if column < 2 and t + 1 >= cycles:
                return set()
            edge = column_of(t, column) // 2 + (1 if t + 1 == cycles else 0)
            return {q for q in range(chips) if q >= edge and q > 0}

        if any(wanted(column) for column in range(cols)):
            mine.append(spread(held[t], wanted, (0, 1)))
            other.append(trade(mine[-1], wanted))
    tiles = len(mine)

    part = half // 2
    packed = call(
        factor_kernel,
        [(half + SUB, tile)],
        [swapped, own],
        [vmem(*whole)] * 2
        + [vmem(part, part)] * 2
        + [vmem(half, half)] * 2
        + [vmem(part, part), vmem(half, half), copies(2)],
    )[0]

    def everyone(column):
        return set(range(chips))

    corner = jnp.where(c == 0, back, lead)
    for b in range(2, cols):
        corner = jnp.where(c == b, send(lead, [((0, 1), (0, b))]), corner)
    corner = spread(corner, everyone, (0,))
    corner_odd = trade(corner, everyone, (0,))

    piece = packed
    for b in range(cols):
        if b != 1:
            piece = jnp.where(c == b, send(packed, [((1, 1), (1, b))]), piece)
    piece_odd = spread(piece, everyone, (1,))
    piece_even = trade(piece_odd, everyone, (1,))

    product = 2 * tile**3
    panel, near_part, *products = call(
        functools.partial(early_kernel, cols, cycles, tiles),
        [whole] * (2 + 2 * tiles),
        [own, diag_inverse, held[-1], *moved[0], *moved[1], *mine, *other, *held[:tiles]],
        [vmem(*whole)] * 3 + [copies(5)],
        flops=3 * product,
    )
    first_t, partial = products[:tiles], products[tiles:]
    pair, *schur_t = call(
        functools.partial(middle_kernel, cols, tiles),
        [(2 * tile, tile)] + [whole] * tiles,
        [corner, corner_odd, panel, own, back, *moved[0], *moved[1], *mine, *other, *first_t],
        [vmem(*whole)] * 2 + [copies(6)],
        flops=2 * product,
    )
    edges = [column_of(cycles - 1, b) for b in range(2, cols)]
    pairs = [((j, b), (j + 1, b)) for b, j in zip(range(2, cols), edges) if j % 2 == 0]
    near_pair = send(pair, pairs)
    panels, trailing = call(
        functools.partial(late_kernel, cols, cycles, tiles),
        [(tile, 2 * tile // cols), covariance.shape],
        [piece_even, piece_odd, pair, near_pair, held[-1], near_part, *partial, *schur_t],
        [vmem(half + SUB, tile)] + [vmem(2 * tile, tile)] * 2 + [vmem(*whole)] * 2 + [copies(4)],
        flops=2 * product,
    )
    return panels, trailing


def solution(mesh):
    rows, cols = mesh.shape["row"], mesh.shape["col"]

    def body(covariance, diag_inverse):
        return local(covariance, diag_inverse, rows, cols)

    return jax.shard_map(
        body,
        mesh=mesh,
        in_specs=(P("row", None, "col"), P()),
        out_specs=(P("row", "col"), P("row", None, "col")),
        check_vma=False,
    )
```

profile of v0, /device:TPU:23, one launch (start us, length us, event | category | flops | bytes accessed | tf_op | source)
XLA Modules:
  0.0 163.1 jit_solution(16100451457503258242)
XLA Ops:
  0.6 4.7 %shard_map.41 = (f32[512,512]{1,0:T(8,128)}, f32[512,512]{1,0:T(8,128)}, f32[256,512]{1,0:T(8,128)}, f32[256,512]{1,0:T(8,128)}, f32[512,512]{1,0:T(8,128)}, /*index=5*/f32[512,512]{1,0:T(8,128)}) custom-call(f32[512,2,512]{2,1,0:T(2,128)} %cov_ref.1, f32[512,512]{1,0:T(8,128)} %refs_1_.1), custom_call_target="tpu_custom_call" | custom-call | bytes 8388608 | tf_op jit(solution)/shard_map/pallas_call | solution.py:137
  6.8 1.7 %collective-permute-start.8 = (f32[512,512]{1,0:T(8,128)}, f32[512,512]{1,0:T(8,128)}, u32[]{:S(2)}, u32[]{:S(2)}) collective-permute-start(f32[512,512]{1,0:T(8,128)} %get-tuple-element.14), channel_id=1, source_target_pairs={{1,2}} | collective-permute-start | bytes 3145736 | tf_op jit(solution)/shard_map/ppermute | solution.py:449
  8.5 1.7 %collective-permute-start.19 = (f32[512,512]{1,0:T(8,128)}, f32[512,512]{1,0:T(8,128)}, u32[]{:S(2)}, u32[]{:S(2)}) collective-permute-start(f32[512,512]{1,0:T(8,128)} %get-tuple-element.19.refs_11_), channel_id=1, source_target_pairs={{0,8},{1,9},{2,10},{3,11},{4,20},{5,21},{6,22},{7,23}} | collective-permute-start | bytes 3145736 | tf_op jit(solution)/shard_map/ppermute | solution.py:449
  11.2 2.1 %select_select_fusion = f32[512,512]{1,0:T(8,128)S(1)} fusion(f32[512,512]{1,0:T(8,128)} %copy-done.9, f32[512,512]{1,0:T(8,128)} %collective-permute-done.8, f32[512,512]{1,0:T(8,128)S(1)} %collective-permute-done.9.refs_4_, f32[512,512]{1,0:T(8,128)} %get-tuple-element.14, pred[]{:T(512)S(6)} %eq.15, pred[]{:T(512)S(6)} %eq.14, pred[]{:T(512)S(6)} %eq.13), kind=kLoop, calls=%fused_computation | loop fusion | flops 786432 | bytes 5242883 | tf_op jit(solution)/shard_map/jit(_where)/select_n | solution.py:546
  13.3 1.7 %collective-permute-start.10 = (f32[512,512]{1,0:T(8,128)S(1)}, f32[512,512]{1,0:T(8,128)}, u32[]{:S(2)}, u32[]{:S(2)}) collective-permute-start(f32[512,512]{1,0:T(8,128)S(1)} %select_select_fusion), channel_id=1, source_target_pairs={{0,8},{1,9},{2,10},{3,11}} | collective-permute-start | bytes 3145736 | tf_op jit(solution)/shard_map/ppermute | solution.py:449
  14.9 1.7 %collective-permute-start = (f32[512,512]{1,0:T(8,128)}, f32[512,512]{1,0:T(8,128)}, u32[]{:S(2)}, u32[]{:S(2)}) collective-permute-start(f32[512,512]{1,0:T(8,128)} %get-tuple-element.14), channel_id=1, source_target_pairs={{1,5}} | collective-permute-start | bytes 3145736 | tf_op jit(solution)/shard_map/ppermute | solution.py:449
  16.6 1.4 broadcast_select_fusion
  18.1 1.3 collective-permute-start.20
  19.6 1.7 %collective-permute-start.11 = (f32[512,512]{1,0:T(8,128)S(1)}, f32[512,512]{1,0:T(8,128)}, u32[]{:S(2)}, u32[]{:S(2)}) collective-permute-start(f32[512,512]{1,0:T(8,128)S(1)} %broadcast_select_fusion.2), channel_id=1, source_target_pairs={{0,16},{8,24},{1,17},{9,25},{2,18},{10,26},{3,19},{11,27}} | collective-permute-start | bytes 3145736 | tf_op jit(solution)/shard_map/ppermute | solution.py:449
  21.3 1.3 collective-permute-start.13
  22.6 1.3 collective-permute-start.16
  23.9 28.8 %collective-permute-done.13.refs_3_.refs_5_ = f32[256,512]{1,0:T(8,128)} collective-permute-done((f32[256,512]{1,0:T(8,128)}, f32[256,512]{1,0:T(8,128)}, u32[]{:S(2)}, u32[]{:S(2)}) %collective-permute-start.13) | collective-permute-done | bytes 524320 | tf_op jit(solution)/shard_map/ppermute | solution.py:449
  52.7 1.9 %collective-permute-start.14 = (f32[256,512]{1,0:T(8,128)}, f32[256,512]{1,0:T(8,128)}, u32[]{:S(2)}, u32[]{:S(2)}) collective-permute-start(f32[256,512]{1,0:T(8,128)} %collective-permute-done.13.refs_3_.refs_5_), channel_id=1, source_target_pairs={{9,10},{13,14},{17,18},{21,22},{25,26},{29,30},{6,7},{10,11},{14,1... | collective-permute-start | bytes 1572872 | tf_op jit(solution)/shard_map/ppermute | solution.py:449
  54.6 9.3 %collective-permute-done.16.refs_6_.refs_8_ = f32[256,512]{1,0:T(8,128)} collective-permute-done((f32[256,512]{1,0:T(8,128)}, f32[256,512]{1,0:T(8,128)}, u32[]{:S(2)}, u32[]{:S(2)}) %collective-permute-start.16) | collective-permute-done | bytes 524320 | tf_op jit(solution)/shard_map/ppermute | solution.py:449
  63.9 1.9 %collective-permute-start.17 = (f32[256,512]{1,0:T(8,128)}, f32[256,512]{1,0:T(8,128)}, u32[]{:S(2)}, u32[]{:S(2)}) collective-permute-start(f32[256,512]{1,0:T(8,128)} %collective-permute-done.16.refs_6_.refs_8_), channel_id=1, source_target_pairs={{9,10},{13,14},{17,18},{21,22},{25,26},{29,30},{6,7},{10,11},{14,1... | collective-permute-start | bytes 1572872 | tf_op jit(solution)/shard_map/ppermute | solution.py:449
  68.3 1.4 broadcast_select_fusion.1.refs_9_.refs_11_
  69.8 7.5 %collective-permute-start.21 = (f32[512,512]{1,0:T(8,128)S(1)}, f32[512,512]{1,0:T(8,128)S(1)}, u32[]{:S(2)}, u32[]{:S(2)}) collective-permute-start(f32[512,512]{1,0:T(8,128)S(1)} %broadcast_select_fusion.1.refs_9_.refs_11_), channel_id=1, source_target_pairs={{16,20},{20,16},{24,28},{28,24},{17,21},{21,17},{25,29},{29,25},{1... | collective-permute-start | bytes 3145736 | tf_op jit(solution)/shard_map/ppermute | solution.py:449
  78.5 1.3 collective-permute-start.12
  79.8 6.6 %collective-permute-done.17.refs_7_.refs_9_ = f32[256,512]{1,0:T(8,128)} collective-permute-done((f32[256,512]{1,0:T(8,128)}, f32[256,512]{1,0:T(8,128)}, u32[]{:S(2)}, u32[]{:S(2)}) %collective-permute-start.17) | collective-permute-done | bytes 524320 | tf_op jit(solution)/shard_map/ppermute | solution.py:449
  87.1 1.3 collective-permute-start.15
  88.5 1.3 collective-permute-start.18
  90.0 1.5 collective-permute-start.4
  91.5 5.8 %collective-permute-done.15.refs_5_.refs_7_ = f32[256,512]{1,0:T(8,128)S(1)} collective-permute-done((f32[256,512]{1,0:T(8,128)}, f32[256,512]{1,0:T(8,128)S(1)}, u32[]{:S(2)}, u32[]{:S(2)}) %collective-permute-start.15) | collective-permute-done | bytes 524320 | tf_op jit(solution)/shard_map/ppermute | solution.py:449
  97.4 11.2 %collective-permute-done.18.refs_8_.refs_10_ = f32[256,512]{1,0:T(8,128)S(1)} collective-permute-done((f32[256,512]{1,0:T(8,128)}, f32[256,512]{1,0:T(8,128)S(1)}, u32[]{:S(2)}, u32[]{:S(2)}) %collective-permute-start.18) | collective-permute-done | bytes 524320 | tf_op jit(solution)/shard_map/ppermute | solution.py:449
  110.4 10.7 %shard_map.43 = (f32[512,512]{1,0:T(8,128)}, f32[512,512]{1,0:T(8,128)}, f32[512,512]{1,0:T(8,128)}, f32[512,512]{1,0:T(8,128)}) custom-call(f32[512,512]{1,0:T(8,128)} %get-tuple-element.15.own_ref.refs_0_.refs_3_, f32[512,512]{1,0:T(8,128)} %refs_1_.1, f32[512,512]{1,0:T(8,128)} %get-tuple-element.16.refs_2_.refs_4_, ...), custom_call_target="tpu_custom_call" | custom-call | flops 805306368 | bytes 13631488 | tf_op jit(solution)/shard_map/pallas_call | solution.py:137
  121.1 8.8 %shard_map.44 = (f32[1024,512]{1,0:T(8,128)}, f32[512,512]{1,0:T(8,128)}) custom-call(f32[512,512]{1,0:T(8,128)} %broadcast_select_fusion.3.refs_0_, f32[512,512]{1,0:T(8,128)} %collective-permute-done.12.refs_1_, f32[512,512]{1,0:T(8,128)} %get-tuple-element.20.refs_2_, f32[512,512]{1,0:T(8,128)} %get-tuple-element.15.own_ref.refs_0_.refs_3_, ...), custom_call_target="tpu_custom_call" | custom-call | flops 536870912 | bytes 14680064 | tf_op jit(solution)/shard_map/pallas_call | solution.py:137
  129.9 1.3 collective-permute-start.22
  132.4 1.3 collective-permute-start.5
  133.7 10.2 %collective-permute-done.5 = f32[264,512]{1,0:T(8,128)} collective-permute-done((f32[264,512]{1,0:T(8,128)S(1)}, f32[264,512]{1,0:T(8,128)}, u32[]{:S(2)}, u32[]{:S(2)}) %collective-permute-start.5) | collective-permute-done | bytes 540704 | tf_op jit(solution)/shard_map/ppermute | solution.py:449
  145.0 1.3 collective-permute-start.6
  146.4 1.5 collective-permute-done.6.refs_0_
  149.3 13.5 %shard_map.45 = (f32[512,256]{1,0:T(8,128)}, f32[512,2,512]{2,1,0:T(2,128)}) custom-call(f32[264,512]{1,0:T(8,128)} %copy-done.10, f32[264,512]{1,0:T(8,128)} %copy-done.4, f32[1024,512]{1,0:T(8,128)} %get-tuple-element.22.refs_2_, f32[1024,512]{1,0:T(8,128)} %copy-done.8, f32[512,512]{1,0:T(8,128)} %get-tuple-element.16.refs_2_.refs_4_, ...), custom_call_target="tpu_custom_call" | custom-call | flops 536870912 | bytes 12091392 | tf_op jit(solution)/shard_map/pallas_call | solution.py:137
  (49 shorter events, 12.7 us)
Async XLA Ops:
  5.4 4.8 %collective-permute-start.9 = (f32[512,512]{1,0:T(8,128)}, f32[512,512]{1,0:T(8,128)S(1)}, u32[]{:S(2)}, u32[]{:S(2)}) collective-permute-start(f32[512,512]{1,0:T(8,128)} %get-tuple-element.14), channel_id=1, source_target_pairs={{1,0},{17,16},{21,20},{25,24},{29,28}} | collective-permute-start | bytes 3145736 | tf_op jit(solution)/shard_map/ppermute | solution.py:449
  6.1 4.1 %collective-permute-start.7 = (f32[512,512]{1,0:T(8,128)}, f32[512,512]{1,0:T(8,128)S(1)}, u32[]{:S(2)}, u32[]{:S(2)}) collective-permute-start(f32[512,512]{1,0:T(8,128)} %get-tuple-element.14), channel_id=1, source_target_pairs={{1,3}} | collective-permute-start | bytes 3145736 | tf_op jit(solution)/shard_map/ppermute | solution.py:449
  6.8 4.3 %collective-permute-start.8 = (f32[512,512]{1,0:T(8,128)}, f32[512,512]{1,0:T(8,128)}, u32[]{:S(2)}, u32[]{:S(2)}) collective-permute-start(f32[512,512]{1,0:T(8,128)} %get-tuple-element.14), channel_id=1, source_target_pairs={{1,2}} | collective-permute-start | bytes 3145736 | tf_op jit(solution)/shard_map/ppermute | solution.py:449
  8.5 8.1 %collective-permute-start.19 = (f32[512,512]{1,0:T(8,128)}, f32[512,512]{1,0:T(8,128)}, u32[]{:S(2)}, u32[]{:S(2)}) collective-permute-start(f32[512,512]{1,0:T(8,128)} %get-tuple-element.19.refs_11_), channel_id=1, source_target_pairs={{0,8},{1,9},{2,10},{3,11},{4,20},{5,21},{6,22},{7,23}} | collective-permute-start | bytes 3145736 | tf_op jit(solution)/shard_map/ppermute | solution.py:449
  10.2 6.4 %copy-start.1 = (f32[512,512]{1,0:T(8,128)S(1)}, f32[512,512]{1,0:T(8,128)}, u32[]{:S(2)}) copy-start(f32[512,512]{1,0:T(8,128)} %get-tuple-element.19.refs_11_) | copy-start | bytes 3145732
  10.2 3.1 %copy-start.3 = (f32[512,512]{1,0:T(8,128)}, f32[512,512]{1,0:T(8,128)S(1)}, u32[]{:S(2)}) copy-start(f32[512,512]{1,0:T(8,128)S(1)} %collective-permute-done.9.refs_4_) | copy-start | bytes 3145732
  10.2 1.0 copy-start.9
  13.3 6.1 %collective-permute-start.10 = (f32[512,512]{1,0:T(8,128)S(1)}, f32[512,512]{1,0:T(8,128)}, u32[]{:S(2)}, u32[]{:S(2)}) collective-permute-start(f32[512,512]{1,0:T(8,128)S(1)} %select_select_fusion), channel_id=1, source_target_pairs={{0,8},{1,9},{2,10},{3,11}} | collective-permute-start | bytes 3145736 | tf_op jit(solution)/shard_map/ppermute | solution.py:449
  14.9 50.9 %collective-permute-start = (f32[512,512]{1,0:T(8,128)}, f32[512,512]{1,0:T(8,128)}, u32[]{:S(2)}, u32[]{:S(2)}) collective-permute-start(f32[512,512]{1,0:T(8,128)} %get-tuple-element.14), channel_id=1, source_target_pairs={{1,5}} | collective-permute-start | bytes 3145736 | tf_op jit(solution)/shard_map/ppermute | solution.py:449
  18.1 49.6 %collective-permute-start.20 = (f32[512,512]{1,0:T(8,128)S(1)}, f32[512,512]{1,0:T(8,128)}, u32[]{:S(2)}, u32[]{:S(2)}) collective-permute-start(f32[512,512]{1,0:T(8,128)S(1)} %broadcast_select_fusion), channel_id=1, source_target_pairs={{0,16},{8,24},{1,17},{9,25},{2,18},{10,26},{3,19},{11,27},{20,28},... | collective-permute-start | bytes 3145736 | tf_op jit(solution)/shard_map/ppermute | solution.py:449
  19.6 50.2 %collective-permute-start.11 = (f32[512,512]{1,0:T(8,128)S(1)}, f32[512,512]{1,0:T(8,128)}, u32[]{:S(2)}, u32[]{:S(2)}) collective-permute-start(f32[512,512]{1,0:T(8,128)S(1)} %broadcast_select_fusion.2), channel_id=1, source_target_pairs={{0,16},{8,24},{1,17},{9,25},{2,18},{10,26},{3,19},{11,27}} | collective-permute-start | bytes 3145736 | tf_op jit(solution)/shard_map/ppermute | solution.py:449
  21.3 31.4 %collective-permute-start.13 = (f32[256,512]{1,0:T(8,128)}, f32[256,512]{1,0:T(8,128)}, u32[]{:S(2)}, u32[]{:S(2)}) collective-permute-start(f32[256,512]{1,0:T(8,128)} %get-tuple-element.17), channel_id=1, source_target_pairs={{0,1},{8,9},{12,13},{16,17},{20,21},{24,25},{28,29},{5,6},{9,10},{... | collective-permute-start | bytes 1572872 | tf_op jit(solution)/shard_map/ppermute | solution.py:449
  22.6 41.4 %collective-permute-start.16 = (f32[256,512]{1,0:T(8,128)}, f32[256,512]{1,0:T(8,128)}, u32[]{:S(2)}, u32[]{:S(2)}) collective-permute-start(f32[256,512]{1,0:T(8,128)} %get-tuple-element.18), channel_id=1, source_target_pairs={{0,1},{8,9},{12,13},{16,17},{20,21},{24,25},{28,29},{5,6},{9,10},{... | collective-permute-start | bytes 1572872 | tf_op jit(solution)/shard_map/ppermute | solution.py:449
  52.7 25.8 %collective-permute-start.14 = (f32[256,512]{1,0:T(8,128)}, f32[256,512]{1,0:T(8,128)}, u32[]{:S(2)}, u32[]{:S(2)}) collective-permute-start(f32[256,512]{1,0:T(8,128)} %collective-permute-done.13.refs_3_.refs_5_), channel_id=1, source_target_pairs={{9,10},{13,14},{17,18},{21,22},{25,26},{29,30},{6,7},{10,11},{14,1... | collective-permute-start | bytes 1572872 | tf_op jit(solution)/shard_map/ppermute | solution.py:449
  63.9 22.5 %collective-permute-start.17 = (f32[256,512]{1,0:T(8,128)}, f32[256,512]{1,0:T(8,128)}, u32[]{:S(2)}, u32[]{:S(2)}) collective-permute-start(f32[256,512]{1,0:T(8,128)} %collective-permute-done.16.refs_6_.refs_8_), channel_id=1, source_target_pairs={{9,10},{13,14},{17,18},{21,22},{25,26},{29,30},{6,7},{10,11},{14,1... | collective-permute-start | bytes 1572872 | tf_op jit(solution)/shard_map/ppermute | solution.py:449
  66.9 20.2 %collective-permute-start.1 = (f32[264,512]{1,0:T(8,128)}, f32[264,512]{1,0:T(8,128)S(1)}, u32[]{:S(2)}, u32[]{:S(2)}) collective-permute-start(f32[264,512]{1,0:T(8,128)} %shard_map.42), channel_id=1, source_target_pairs={{5,7}} | collective-permute-start | bytes 1622024 | tf_op jit(solution)/shard_map/ppermute | solution.py:449
  67.6 20.8 %collective-permute-start.2 = (f32[264,512]{1,0:T(8,128)}, f32[264,512]{1,0:T(8,128)S(1)}, u32[]{:S(2)}, u32[]{:S(2)}) collective-permute-start(f32[264,512]{1,0:T(8,128)} %shard_map.42), channel_id=1, source_target_pairs={{5,6}} | collective-permute-start | bytes 1622024 | tf_op jit(solution)/shard_map/ppermute | solution.py:449
  69.8 20.3 %copy-start = (f32[512,512]{1,0:T(8,128)}, f32[512,512]{1,0:T(8,128)S(1)}, u32[]{:S(2)}) copy-start(f32[512,512]{1,0:T(8,128)S(1)} %broadcast_select_fusion.1.refs_9_.refs_11_) | copy-start | bytes 3145732
  69.8 16.6 %copy-start.5 = (f32[264,512]{1,0:T(8,128)S(1)}, f32[264,512]{1,0:T(8,128)}, u32[]{:S(2)}) copy-start(f32[264,512]{1,0:T(8,128)} %shard_map.42) | copy-start | bytes 1622020
  69.8 38.8 %collective-permute-start.21 = (f32[512,512]{1,0:T(8,128)S(1)}, f32[512,512]{1,0:T(8,128)S(1)}, u32[]{:S(2)}, u32[]{:S(2)}) collective-permute-start(f32[512,512]{1,0:T(8,128)S(1)} %broadcast_select_fusion.1.refs_9_.refs_11_), channel_id=1, source_target_pairs={{16,20},{20,16},{24,28},{28,24},{17,21},{21,17},{25,29},{29,25},{1... | collective-permute-start | bytes 3145736 | tf_op jit(solution)/shard_map/ppermute | solution.py:449
  78.5 42.6 %collective-permute-start.12 = (f32[512,512]{1,0:T(8,128)}, f32[512,512]{1,0:T(8,128)}, u32[]{:S(2)}, u32[]{:S(2)}) collective-permute-start(f32[512,512]{1,0:T(8,128)} %broadcast_select_fusion.3.refs_0_), channel_id=1, source_target_pairs={{0,4},{8,12},{16,20},{24,28},{1,5},{9,13},{17,21},{25,29},{2,6},{1... | collective-permute-start | bytes 3145736 | tf_op jit(solution)/shard_map/ppermute | solution.py:449
  86.4 3.4 %collective-permute-start.3 = (f32[264,512]{1,0:T(8,128)S(1)}, f32[264,512]{1,0:T(8,128)S(1)}, u32[]{:S(2)}, u32[]{:S(2)}) collective-permute-start(f32[264,512]{1,0:T(8,128)S(1)} %copy-done.5), channel_id=1, source_target_pairs={{5,4}} | collective-permute-start | bytes 1622024 | tf_op jit(solution)/shard_map/ppermute | solution.py:449
  87.1 10.2 %collective-permute-start.15 = (f32[256,512]{1,0:T(8,128)}, f32[256,512]{1,0:T(8,128)S(1)}, u32[]{:S(2)}, u32[]{:S(2)}) collective-permute-start(f32[256,512]{1,0:T(8,128)} %collective-permute-done.14.refs_4_.refs_6_), channel_id=1, source_target_pairs={{10,11},{14,15},{18,19},{22,23},{26,27},{30,31}} | collective-permute-start | bytes 1572872 | tf_op jit(solution)/shard_map/ppermute | solution.py:449
  88.5 20.1 %collective-permute-start.18 = (f32[256,512]{1,0:T(8,128)}, f32[256,512]{1,0:T(8,128)S(1)}, u32[]{:S(2)}, u32[]{:S(2)}) collective-permute-start(f32[256,512]{1,0:T(8,128)} %collective-permute-done.17.refs_7_.refs_9_), channel_id=1, source_target_pairs={{10,11},{14,15},{18,19},{22,23},{26,27},{30,31}} | collective-permute-start | bytes 1572872 | tf_op jit(solution)/shard_map/ppermute | solution.py:449
  90.0 41.2 %collective-permute-start.4 = (f32[264,512]{1,0:T(8,128)S(1)}, f32[264,512]{1,0:T(8,128)}, u32[]{:S(2)}, u32[]{:S(2)}) collective-permute-start(f32[264,512]{1,0:T(8,128)S(1)} %select_select_fusion.1), channel_id=1, source_target_pairs={{4,20},{5,21},{6,22},{7,23}} | collective-permute-start | bytes 1622024 | tf_op jit(solution)/shard_map/ppermute | solution.py:449
  97.4 11.2 %copy-start.6 = (f32[256,512]{1,0:T(8,128)}, f32[256,512]{1,0:T(8,128)S(1)}, u32[]{:S(2)}) copy-start(f32[256,512]{1,0:T(8,128)S(1)} %collective-permute-done.15.refs_5_.refs_7_) | copy-start | bytes 1572868
  109.4 1.0 copy-start.2
  129.9 18.0 %collective-permute-start.22 = (f32[1024,512]{1,0:T(8,128)}, f32[1024,512]{1,0:T(8,128)S(1)}, u32[]{:S(2)}, u32[]{:S(2)}) collective-permute-start(f32[1024,512]{1,0:T(8,128)} %get-tuple-element.22.refs_2_), channel_id=1, source_target_pairs={{26,30}} | collective-permute-start | bytes 6291464 | tf_op jit(solution)/shard_map/ppermute | solution.py:449
  132.4 11.5 %collective-permute-start.5 = (f32[264,512]{1,0:T(8,128)S(1)}, f32[264,512]{1,0:T(8,128)}, u32[]{:S(2)}, u32[]{:S(2)}) collective-permute-start(f32[264,512]{1,0:T(8,128)S(1)} %broadcast_select_fusion.4), channel_id=1, source_target_pairs={{4,12},{20,28},{5,13},{21,29},{6,14},{22,30},{7,15},{23,31}} | collective-permute-start | bytes 1622024 | tf_op jit(solution)/shard_map/ppermute | solution.py:449
  145.0 2.9 %copy-start.4 = (f32[264,512]{1,0:T(8,128)}, f32[264,512]{1,0:T(8,128)S(1)}, u32[]{:S(2)}) copy-start(f32[264,512]{1,0:T(8,128)S(1)} %broadcast_select_fusion.5.refs_1_) | copy-start | bytes 1622020
  145.0 2.8 %collective-permute-start.6 = (f32[264,512]{1,0:T(8,128)S(1)}, f32[264,512]{1,0:T(8,128)S(1)}, u32[]{:S(2)}, u32[]{:S(2)}) collective-permute-start(f32[264,512]{1,0:T(8,128)S(1)} %broadcast_select_fusion.5.refs_1_), channel_id=1, source_target_pairs={{4,0},{12,8},{20,16},{28,24},{5,1},{13,9},{21,17},{29,25},{6,2},{1... | collective-permute-start | bytes 1622024 | tf_op jit(solution)/shard_map/ppermute | solution.py:449
  147.9 1.5 copy-start.8
  (2 other events, 1.6 us)
where the time goes:
time: 164 us; the launch traced here: 163 us
  waiting for transfers between devices  73.6 us (45%)
  Pallas kernels  38.8 us (24%)
  starting transfers between devices  36.4 us (22%)
  other arithmetic  8.87 us (5%)
  local copies, waits for them, and re-layouts  4.25 us (3%)
    ppermute x23, waiting for transfers between devices, send(): return lax.ppermute(value, AXES, flat)  73.6 us
    pallas_call x5, Pallas kernels, call(): pl.pallas_call(kernel, out_shape=outs, in_specs=[pl.BlockSpec(memory_spac...  38.8 us
    ppermute x23, starting transfers between devices, send(): return lax.ppermute(value, AXES, flat)  36.4 us
    select_n x6, other arithmetic, spread(): current = jnp.where(arrived, send(current, pairs), current)  6.56 us
    unnamed x22, local copies, waits for them, and re-layouts  4.25 us
  transfers between devices with their start and end apart: 23, of which 7 were waited for; matrix products, arithmetic and copies ran while one was open for 5% of the time, Pallas kernels for 13%

commit v1 on v0

v1 whole, which is shorter than its diff:
```python
import functools

import jax
import jax.numpy as jnp
from jax import lax
from jax.experimental import pallas as pl
from jax.experimental.pallas import tpu as pltpu
from jax.sharding import PartitionSpec as P

HIGHEST = lax.Precision.HIGHEST
AXES = ("row", "col")
SUB = 8


def dot(left, right, lhs_dim, rhs_dim):
    return lax.dot_general(
        left,
        right,
        (((lhs_dim,), (rhs_dim,)), ((), ())),
        precision=HIGHEST,
        preferred_element_type=jnp.float32,
    )


def nn(left, right):
    return dot(left, right, 1, 0)


def nt(left, right):
    return dot(left, right, 1, 1)


def tn(left, right):
    return dot(left, right, 0, 0)


def halves(value):
    high = value.astype(jnp.bfloat16)
    return high, (value - high.astype(jnp.float32)).astype(jnp.bfloat16)


def dot3(left, right, lhs_dim, rhs_dim):
    (a, b), (x, y) = halves(left), halves(right)

    def part(u, v):
        return lax.dot_general(
            u, v, (((lhs_dim,), (rhs_dim,)), ((), ())), preferred_element_type=jnp.float32
        )

    return part(a, x) + (part(a, y) + part(b, x))


def factor_block(work, aug):
    size = work.shape[0]
    groups = size // SUB
    rows = lax.broadcasted_iota(jnp.int32, (SUB, size), 0)
    lanes = lax.broadcasted_iota(jnp.int32, (SUB, size), 1)
    for t in range(groups):
        aug[t * SUB : (t + 1) * SUB, :] = jnp.where(lanes == rows + t * SUB, 1.0, 0.0)

    def lane(value, index):
        return jnp.broadcast_to(value[:, index : index + 1], (SUB, size))

    def row(value, index):
        return jnp.broadcast_to(value[index : index + 1, :], (SUB, size))

    for s in range(groups):
        here = slice(s * SUB, (s + 1) * SUB)
        own, own_aug = work[here, :], aug[here, :]
        columns = [lane(own, s * SUB + b) for b in range(SUB)]
        small = [[row(columns[b], a) if a >= b else None for b in range(SUB)] for a in range(SUB)]
        upper = [row(own, i) for i in range(SUB)]
        inverse = [row(own_aug, i) for i in range(SUB)]
        low = [[None] * SUB for _ in range(SUB)]
        scale = []
        for i in range(SUB):
            scale.append(lax.rsqrt(small[i][i]))
            for a in range(i + 1, SUB):
                low[a][i] = small[a][i] * scale[i]
            for b in range(i + 1, SUB):
                for a in range(b, SUB):
                    small[a][b] = small[a][b] - low[a][i] * low[b][i]
            upper[i] = upper[i] * scale[i]
            inverse[i] = inverse[i] * scale[i]
            for b in range(i + 1, SUB):
                upper[b] = upper[b] - upper[i] * low[b][i]
                inverse[b] = inverse[b] - inverse[i] * low[b][i]
        for t in range(s + 1, groups):
            there = slice(t * SUB, (t + 1) * SUB)
            current, current_aug = work[there, :], aug[there, :]
            part = [lane(current, s * SUB + b) for b in range(SUB)]
            for i in range(SUB):
                part[i] = part[i] * scale[i]
                for b in range(i + 1, SUB):
                    part[b] = part[b] - part[i] * low[b][i]
                current = current - part[i] * upper[i]
                current_aug = current_aug - part[i] * inverse[i]
            work[there, :] = current
            aug[there, :] = current_aug
        packed = inverse[0]
        for i in range(1, SUB):
            packed = jnp.where(rows == i, inverse[i], packed)
        aug[here, :] = packed


def masks(shape):
    return lax.broadcasted_iota(jnp.int32, shape, 0), lax.broadcasted_iota(jnp.int32, shape, 1)


def unpack(packed):
    half = packed.shape[1] // 2
    block = packed[:half, :half]
    rows, lanes = masks(block.shape)
    diag = jnp.broadcast_to(packed[half : half + 1, :half], block.shape)
    first = jnp.where(lanes <= rows, block, 0.0)
    second_t = jnp.where(lanes > rows, block, jnp.where(lanes == rows, diag, 0.0))
    return first, packed[:half, half:], second_t


def place():
    return lax.axis_index("row"), lax.axis_index("col")


def fetch(target, semaphore, choices):
    for condition, source in choices:

        @pl.when(condition)
        def _(source=source):
            pltpu.make_async_copy(source, target, semaphore).start()

    return pltpu.make_async_copy(choices[0][1], target, semaphore).wait


def call(kernel, out_shapes, inputs, scratch, vmem_inputs=(), flops=0):
    outs = [jax.ShapeDtypeStruct(shape, jnp.float32) for shape in out_shapes]
    size = sum(4 * x.size for x in inputs) + sum(4 * x.size for x in outs)
    return pl.pallas_call(
        kernel,
        out_shape=outs,
        in_specs=[
            pl.BlockSpec(memory_space=pltpu.VMEM if i in vmem_inputs else pltpu.HBM)
            for i in range(len(inputs))
        ],
        out_specs=[pl.BlockSpec(memory_space=pltpu.VMEM)] * len(outs),
        scratch_shapes=scratch,
        cost_estimate=pl.CostEstimate(flops=flops, bytes_accessed=size, transcendentals=0),
    )(*inputs)


def vmem(*shape):
    return pltpu.VMEM(shape, jnp.float32)


def copies(count):
    return pltpu.SemaphoreType.DMA((count,))


def split(refs, *counts):
    groups = []
    for count in counts:
        groups.append(refs[:count])
        refs = refs[count:]
    return groups


def extract_kernel(cov_ref, diag_ref, lead_ref, low_ref, high_ref, *refs):
    held_refs, dinv, sems = refs[:-2], refs[-2], refs[-1]
    half = low_ref.shape[0]
    cycles = cov_ref.shape[1]
    r, c = place()
    source = (r == 0) & (c == 1)

    @pl.when(source)
    def _():
        pltpu.make_async_copy(diag_ref, dinv, sems.at[0]).start()

    own = cov_ref[:, 0, :]
    lead_ref[...] = own
    low_ref[...] = own[:half]
    high_ref[...] = own[half:]
    for t, held_ref in enumerate(held_refs):
        later = cov_ref[:, min(t + 1, cycles - 1), :]
        held_ref[...] = jnp.where(c < 2, later, cov_ref[:, t, :])

    @pl.when(source)
    def _():
        pltpu.make_async_copy(diag_ref, dinv, sems.at[0]).wait()
        lead_ref[...] = nn(dinv[...], lead_ref[...])


def factor_kernel(corner_ref, own_ref, out_ref, second, diag, aug, first, last, cross, wide, sems):
    half = first.shape[0]
    part = half // 2
    r, c = place()
    owner = (r == 1) & (c == 1)
    a, b, low, high = slice(0, part), slice(part, half), slice(0, half), slice(half, 2 * half)

    @pl.when(owner)
    def _():
        fetch(second, sems.at[0], [(owner, own_ref)])()
        second[...] = second[...] - tn(corner_ref[...], corner_ref[...])
        diag[...] = second[a, a]

        def upper_stage(inverse, base):
            inv = aug[...]
            inverse[a, a] = inv
            inverse[a, b] = jnp.zeros_like(inv)
            rows = slice(base, base + part)
            later = slice(base + part, base + half)
            cross[...] = nn(inv, second[rows, later])
            diag[...] = second[later, later] - tn(cross[...], cross[...])

        def lower_stage(inverse):
            inv = aug[...]
            inverse[b, b] = inv
            inverse[b, a] = -nn(inv, tn(cross[...], inverse[a, a]))

        def step(k, carry):
            factor_block(diag, aug)

            @pl.when(k == 0)
            def _():
                upper_stage(first, 0)

            @pl.when(k == 1)
            def _():
                lower_stage(first)
                wide[...] = nn(first[...], second[low, high])
                second[high, high] = second[high, high] - tn(wide[...], wide[...])
                diag[...] = second[half : half + part, half : half + part]

            @pl.when(k == 2)
            def _():
                upper_stage(last, half)

            @pl.when(k == 3)
            def _():
                lower_stage(last)

            return carry

        lax.fori_loop(0, 4, step, 0)
        inv = last[...]
        rows, lanes = masks(inv.shape)
        out_ref[:half, :half] = jnp.where(lanes <= rows, first[...], inv.T)
        out_ref[:half, half:] = -nn(inv, tn(wide[...], first[...]))
        diagonal = jnp.sum(jnp.where(lanes == rows, inv, 0.0), axis=0, keepdims=True)
        out_ref[half:, :half] = jnp.broadcast_to(diagonal, (SUB, half))
        out_ref[half:, half:] = jnp.zeros((SUB, half), jnp.float32)


def row_choices(cols, which, half, own, parts, back=None):
    _, c = place()
    rows = pl.ds(which * half, half)
    if back is None:
        return [(c == 0, own.at[rows])] + [(c == b, parts[b - 1]) for b in range(1, cols)]
    choices = [(c == 0, back.at[rows]), (c == 1, own.at[rows])]
    return choices + [(c == b, parts[b - 2]) for b in range(2, cols)]


def panel_kernel(cols, cycles, tiles, *refs):
    hops = cols - 1
    (own, back, diag, near_held), low, high, mine, other, held, (pair_ref, near_ref), first_t, part, rest = split(
        refs, 4, hops, hops - 1, tiles, tiles, tiles, 2, tiles, tiles, 2
    )
    dinv, sems = rest
    half = low[0].shape[0]
    r, c = place()
    core = r % 2
    always = c >= 0
    full = c < cols - 1
    top, bottom = slice(0, half), slice(half, 2 * half)
    waits = [
        fetch(dinv, sems.at[0], [(always, diag)]),
        fetch(pair_ref.at[top], sems.at[1], row_choices(cols, 0, half, own, low)),
        fetch(near_ref, sems.at[2], [(always, near_held)]),
    ]
    for i, parts in enumerate((low, high)):
        choices = row_choices(cols, i, half, own, parts, back)
        waits.append(fetch(pair_ref.at[pl.ds((2 + i) * half, half)], sems.at[3 + i], choices))
    for t in range(tiles):
        choices = [(core == 0, mine[t]), (core == 1, other[t])]
        waits.append(fetch(first_t[t], sems.at[6 + 2 * t], choices))
        waits.append(fetch(part[t], sems.at[7 + 2 * t], [(always, held[t])]))

    @pl.when(full)
    def _():
        fetch(pair_ref.at[bottom], sems.at[5], row_choices(cols - 1, 1, half, own, high))()

    for wait in waits:
        wait()

    def wanted(t):
        return r >= (t + jnp.where(c < 2, 1, 0)) * cols + c

    for t in range(tiles):

        @pl.when(wanted(t))
        def _(t=t):
            first_t[t][...] = nn(dinv[...], first_t[t][...])

    def rows_of(i, carry):
        rows = pl.ds(pl.multiple_of(i * half, half), half)
        pair_ref[rows, :] = nt(pair_ref[rows, :], dinv[...])
        for t in range(tiles):

            @pl.when(wanted(t))
            def _(t=t):
                part[t][rows, :] = part[t][rows, :] - nn(pair_ref[rows, :], first_t[t][...])

        return carry

    lax.fori_loop(0, jnp.where(full, 2, 1), rows_of, 0)

    @pl.when(full & (c >= 2) & (r == (cycles - 1) * cols + c))
    def _():
        tile = slice(0, 2 * half)
        near_ref[...] = near_ref[...] - nt(pair_ref[tile, :], pair_ref[tile, :])


def final_kernel(cols, cycles, tiles, *refs):
    (corner_odd, piece_even, corner_even, piece_odd, pair, near_pair, held, near_part, last_rows, diag), arrivals, first_t, mine, other, partial, outs, rest = split(
        refs, 10, cols // 2, tiles, tiles, tiles, tiles, 2, 8
    )
    panels_ref, trailing_ref = outs
    packed, corner, stacks, first, second, total, near_total, sems = rest
    stack, near_stack = stacks.at[0], stacks.at[1]
    tile = near_total.shape[0]
    half = tile // 2
    low, high = slice(0, half), slice(half, tile)
    top, bottom = slice(0, tile), slice(tile, 2 * tile)
    r, c = place()
    core = r % 2
    always = c >= 0
    last = (cycles - 1) * cols + c
    own = (c >= 2) & (r == last)
    near = (c >= 2) & (r == last + 1) & (r // 2 == last // 2)
    late = c == cols - 1

    def wanted(t):
        found = r >= (t + jnp.where(c < 2, 1, 0)) * cols + c
        return found & jnp.logical_not(own | near) if t + 1 == cycles else found

    mine_late = own & late

    @pl.when(near)
    def _():
        pltpu.make_async_copy(near_pair, near_stack, sems.at[1]).start()

    @pl.when(own | near)
    def _():
        fetch(near_total, sems.at[2], [(own & (c < cols - 1), near_part), (near | mine_late, held)])

    @pl.when(late)
    def _():
        pltpu.make_async_copy(diag, near_stack.at[top], sems.at[1]).start()
        pltpu.make_async_copy(pair.at[low], stack.at[low], sems.at[0]).start()
        pltpu.make_async_copy(pair.at[bottom], stack.at[bottom], sems.at[4]).start()
        pltpu.make_async_copy(last_rows, stack.at[high], sems.at[5]).start()

    @pl.when(jnp.logical_not(late))
    def _():
        pltpu.make_async_copy(pair, stack, sems.at[0]).start()

    waits = []
    for t in range(tiles):
        waits.append(fetch(first.at[t], sems.at[6 + 3 * t], [(always, first_t[t])]))
        choices = [(core == 1, mine[t]), (core == 0, other[t])]
        waits.append(fetch(second.at[t], sems.at[7 + 3 * t], choices))
        waits.append(fetch(total.at[t], sems.at[8 + 3 * t], [(always, partial[t])]))

    @pl.when(core == 0)
    def _():
        fetch(corner, sems.at[3], [(always, corner_even)])()
        packed[...] = piece_even[...]

    @pl.when(core == 1)
    def _():
        fetch(packed, sems.at[3], [(always, piece_odd)])()
        corner[...] = corner_odd[...]

    @pl.when(near)
    def _():
        pltpu.make_async_copy(near_pair, near_stack, sems.at[1]).wait()

    @pl.when(own | near)
    def _():
        pltpu.make_async_copy(held, near_total, sems.at[2]).wait()

    @pl.when(jnp.logical_not(late))
    def _():
        pltpu.make_async_copy(pair, stack, sems.at[0]).wait()

    for wait in waits:
        wait()

    @pl.when(late)
    def _():
        pltpu.make_async_copy(diag, near_stack.at[top], sems.at[1]).wait()
        pltpu.make_async_copy(pair.at[low], stack.at[low], sems.at[0]).wait()
        pltpu.make_async_copy(pair.at[bottom], stack.at[bottom], sems.at[4]).wait()
        pltpu.make_async_copy(last_rows, stack.at[high], sems.at[5]).wait()
        stack[high, :] = nt(stack[high, :], near_stack[top, :])
        for t in range(tiles):

            @pl.when(wanted(t))
            def _(t=t):
                total[t, high] = total[t, high] - nn(stack[high, :], first[t])

    @pl.when(r == 1)
    def _():
        stack[top, :] = corner[...].T
        for b, source in zip(range(cols // 2, cols), arrivals):

            @pl.when(c == b)
            def _(source=source):
                fetch(stack.at[bottom], sems.at[3], [(always, source)])()

    g_first, g_below, g_second_t = unpack(packed[...])

    def solve(i, carry):
        @pl.when((i == 0) | near)
        def _():
            target = stacks.at[i]
            target[bottom, :] = target[bottom, :] - nn(target[top, :], corner[...])
            left, right = target[bottom, low], target[bottom, high]
            target[bottom, low] = dot3(left, g_first, 1, 1)
            target[bottom, high] = dot3(left, g_below, 1, 1) + dot3(right, g_second_t, 1, 0)

        return carry

    lax.fori_loop(0, 2, solve, 0)

    @pl.when(r == 0)
    def _():
        stack[bottom, :] = jnp.zeros((tile, tile), jnp.float32)

    width = panels_ref.shape[1]
    for b in range(cols):

        @pl.when(c == b)
        def _(b=b):
            rows, start = (top, b * width) if 2 * b < cols else (bottom, b * width - tile)
            panels_ref[...] = stack[rows, start : start + width]

    trailing_ref[...] = jnp.zeros_like(trailing_ref)

    def store(t, value):
        for shift in (0, 1):
            if t + shift < cycles:

                @pl.when((c < 2) if shift else (c >= 2))
                def _(slot=t + shift):
                    trailing_ref[:, slot, :] = value

    for t in range(tiles):

        @pl.when(wanted(t))
        def _(t=t):
            second[t] = second[t] - tn(corner[...], first[t])
            upper, lower = second[t, low], second[t, high]
            second[t, low] = dot3(g_first, upper, 1, 0)
            second[t, high] = dot3(g_below, upper, 1, 0) + dot3(g_second_t, lower, 0, 0)
            store(t, total[t] - dot3(stack[bottom, :], second[t], 1, 0))

    @pl.when(own)
    def _():
        near_stack[...] = stack[...]

    @pl.when(near | (own & late))
    def _():
        near_total[...] = near_total[...] - nt(stack[top, :], near_stack[top, :])

    @pl.when(own | near)
    def _():
        store(cycles - 1, near_total[...] - dot3(stack[bottom, :], near_stack[bottom, :], 1, 1))


def local(covariance, diag_inverse, rows, cols):
    tile = covariance.shape[0]
    cycles = covariance.shape[1]
    half = tile // 2
    chips = rows // 2
    r, c = place()
    chip, core = r // 2, r % 2
    whole = (tile, tile)

    def send(value, pairs):
        flat = [(a * cols + b, x * cols + y) for (a, b), (x, y) in pairs]
        return lax.ppermute(value, AXES, flat)

    bits = []
    while (1 << len(bits)) < chips:
        bits.append(1 << len(bits))

    def column_of(t, column):
        return (t + (1 if column < 2 else 0)) * cols + column

    lead, own_low, own_high, *held = call(
        extract_kernel,
        [whole, (half, tile), (half, tile)] + [whole] * cycles,
        [covariance, diag_inverse],
        [vmem(*whole), copies(1)],
        vmem_inputs=(0,),
    )

    swapped = send(lead, [((0, 1), (1, 1))])

    def along(column, hop):
        source = column - hop
        return [
            ((a, column), (a, column + 1))
            for a in range(rows)
            if (a >= 2 and source in (0, 1)) or (a == 0 and source == 0 and hop == 0)
        ]

    moved = []
    for part in (own_low, own_high):
        chain = []
        for hop in range(cols - 1):
            pairs = [pair for column in range(cols - 1) for pair in along(column, hop)]
            part = send(part, pairs)
            chain.append(part)
        moved.append(chain)
    back = send(lead, [((a, 1), (a, 0)) for a in range(rows) if a == 0 or a >= min(cols, rows - 1)])

    def spread(value, wanted, cores, extra=()):
        current, arrivals = value, []
        for step in range(len(bits)):
            pairs = list(extra[step : step + 1])
            arrived = False
            for k in cores:
                order = bits if k == 0 else bits[::-1]
                used, bit, later = sum(order[:step]), order[step], sum(order[step + 1 :])
                arrived = jnp.where(core == k, (chip & bit) != 0, arrived)
                for column in range(cols):
                    for q in range(chips):
                        target = q | bit
                        if q & ~used or target >= chips:
                            continue
                        reach = {target | more for more in range(chips) if not more & ~later}
                        if reach & wanted(column):
                            pairs.append(((2 * q + k, column), (2 * target + k, column)))
            if pairs:
                arrivals.append(send(current, pairs))
                current = jnp.where(arrived, arrivals[-1], current)
        return current, arrivals

    def trade(value, wanted, ways=(0, 1)):
        pairs = []
        for column in range(cols):
            for q in wanted(column):
                pairs += [((2 * q + k, column), (2 * q + 1 - k, column)) for k in ways]
        return send(value, pairs)

    mine, other = [], []
    for t in range(cycles):

        def wanted(column, t=t):
            if column < 2 and t + 1 >= cycles:
                return set()
            edge = column_of(t, column) // 2 + (1 if t + 1 == cycles else 0)
            return {q for q in range(chips) if q >= edge and q > 0}

        if any(wanted(column) for column in range(cols)):
            mine.append(spread(held[t], wanted, (0, 1))[0])
            other.append(trade(mine[-1], wanted))
    tiles = len(mine)

    part = half // 2
    packed = call(
        factor_kernel,
        [(half + SUB, tile)],
        [swapped, lead],
        [vmem(*whole)]
        + [vmem(part, part)] * 2
        + [vmem(half, half)] * 2
        + [vmem(part, part), vmem(half, half), copies(1)],
        vmem_inputs=(0,),
    )[0]

    def everyone(column):
        return set(range(chips))

    corner, passed = jnp.where(c == 0, back, lead), lead
    for b in range(2, cols):
        passed = send(passed, [((0, b - 1), (0, b))])
        corner = jnp.where(c == b, passed, corner)
    extra = [((1, 1), (1, b)) for b in range(cols // 2, cols)]
    corner, arrivals = spread(corner, everyone, (0,), extra)
    corner_odd = trade(corner, everyone, (0,))

    piece = packed
    for b in range(cols):
        if b != 1:
            piece = jnp.where(c == b, send(packed, [((1, 1), (1, b))]), piece)
    piece_odd, _ = spread(piece, everyone, (1,))
    piece_even = trade(piece_odd, everyone, (1,))

    product = 2 * tile**3
    pair, near_part, *products = call(
        functools.partial(panel_kernel, cols, cycles, tiles),
        [(2 * tile, tile), whole] + [whole] * (2 * tiles),
        [
            lead, back, diag_inverse, held[-1],
            *moved[0], *moved[1][:-1], *mine, *other, *held[:tiles],
        ],
        [vmem(*whole), copies(6 + 2 * tiles)],
        flops=3 * product,
    )
    first_t, partial = products[:tiles], products[tiles:]
    edges = [column_of(cycles - 1, b) for b in range(2, cols)]
    pairs = [((j, b), (j + 1, b)) for b, j in zip(range(2, cols), edges) if j % 2 == 0]
    near_pair = send(pair, pairs)
    rows_of_one = cols // 2
    panels, trailing = call(
        functools.partial(final_kernel, cols, cycles, tiles),
        [(tile, 2 * tile // cols), covariance.shape],
        [
            corner_odd, piece_even, corner, piece_odd, pair, near_pair, held[-1], near_part,
            moved[1][-1], diag_inverse, *arrivals[:rows_of_one],
            *first_t, *mine, *other, *partial,
        ],
        [vmem(half + SUB, tile), vmem(*whole), vmem(2, 2 * tile, tile)]
        + [vmem(tiles, *whole)] * 3
        + [vmem(*whole), copies(6 + 3 * tiles)],
        vmem_inputs=(0, 1),
        flops=5 * product,
    )
    return panels, trailing


def solution(mesh):
    rows, cols = mesh.shape["row"], mesh.shape["col"]

    def body(covariance, diag_inverse):
        return local(covariance, diag_inverse, rows, cols)

    return jax.shard_map(
        body,
        mesh=mesh,
        in_specs=(P("row", None, "col"), P()),
        out_specs=(P("row", "col"), P("row", None, "col")),
        check_vma=False,
    )
```

time: 164 us -> 145 us (0.88)
  waiting for transfers between devices: 73.6 us -> 54.4 us
  other arithmetic: 8.87 us -> 13.2 us
  starting transfers between devices: 36.4 us -> 33.3 us
  Pallas kernels: 38.8 us -> 36.9 us
    ppermute x23, waiting for transfers between devices: 73.6 us -> 54.4 us  [send(): return lax.ppermute(value, AXES, flat)]
    select_n x7, other arithmetic: 8.64 us -> 13 us  [the longest x6 9.97 us: spread(): current = jnp.where(arrived, arrivals[-1], current)]
    ppermute x23, starting transfers between devices: 36.4 us -> 33.3 us  [send(): return lax.ppermute(value, AXES, flat)]
    pallas_call x5 -> x4, Pallas kernels: 38.8 us -> 36.9 us  [call(): pl.pallas_call(kernel, out_shape=outs, in_specs=[pl.BlockSpec(memory_spac...]
    unnamed x22 -> x28, local copies, waits for them, and re-layouts: 4.25 us -> 4.59 us
  transfers between devices with their start and end apart: 23 -> 23, of which waited for: 7 -> 8; matrix products, arithmetic and copies ran while one was open for 5% -> 9% of each run, Pallas kernels for 13% -> 9%
where the time goes in v1:
time: 145 us; the launch traced here: 144 us
  waiting for transfers between devices  54.4 us (38%)
  Pallas kernels  36.9 us (25%)
  starting transfers between devices  33.3 us (23%)
  other arithmetic  13.2 us (9%)
  local copies, waits for them, and re-layouts  4.59 us (3%)
    ppermute x23, waiting for transfers between devices, send(): return lax.ppermute(value, AXES, flat)  54.4 us
    pallas_call x4, Pallas kernels, call(): pl.pallas_call(kernel, out_shape=outs, in_specs=[pl.BlockSpec(memory_spac...  36.9 us
    ppermute x23, starting transfers between devices, send(): return lax.ppermute(value, AXES, flat)  33.3 us
    select_n x6, other arithmetic, spread(): current = jnp.where(arrived, arrivals[-1], current)  9.97 us
    unnamed x28, local copies, waits for them, and re-layouts  4.59 us
    select_n x1, other arithmetic, local(): corner = jnp.where(c == b, passed, corner)  3.05 us
  transfers between devices with their start and end apart: 23, of which 8 were waited for; matrix products, arithmetic and copies ran while one was open for 9% of the time, Pallas kernels for 9%

profile of v1, /device:TPU:23, one launch (start us, length us, event | category | flops | bytes accessed | tf_op | source)
XLA Modules:
  0.0 143.7 jit_solution(11679800559545866736)
XLA Ops:
  0.6 4.4 %shard_map.41 = (f32[512,512]{1,0:T(8,128)}, f32[256,512]{1,0:T(8,128)}, f32[256,512]{1,0:T(8,128)}, f32[512,512]{1,0:T(8,128)}, f32[512,512]{1,0:T(8,128)}) custom-call(f32[512,2,512]{2,1,0:T(2,128)} %cov_ref.1, f32[512,512]{1,0:T(8,128)} %refs_9_.1), custom_call_target="tpu_custom_call" | custom-call | bytes 7340032 | tf_op jit(solution)/shard_map/pallas_call | solution.py:137
  5.0 1.8 %collective-permute-start = (f32[512,512]{1,0:T(8,128)}, f32[512,512]{1,0:T(8,128)}, u32[]{:S(2)}, u32[]{:S(2)}) collective-permute-start(f32[512,512]{1,0:T(8,128)} %get-tuple-element.11.own_ref.refs_0_), channel_id=1, source_target_pairs={{1,2}} | collective-permute-start | bytes 3145736 | tf_op jit(solution)/shard_map/ppermute | solution.py:490
  6.8 1.6 %collective-permute-start.18 = (f32[512,512]{1,0:T(8,128)}, f32[512,512]{1,0:T(8,128)}, u32[]{:S(2)}, u32[]{:S(2)}) collective-permute-start(f32[512,512]{1,0:T(8,128)} %get-tuple-element.15.refs_11_), channel_id=1, source_target_pairs={{0,8},{1,9},{2,10},{3,11},{4,20},{5,21},{6,22},{7,23}} | collective-permute-start | bytes 3145736 | tf_op jit(solution)/shard_map/ppermute | solution.py:490
  9.2 1.6 %collective-permute-start.1 = (f32[512,512]{1,0:T(8,128)}, f32[512,512]{1,0:T(8,128)}, u32[]{:S(2)}, u32[]{:S(2)}) collective-permute-start(f32[512,512]{1,0:T(8,128)} %collective-permute-done), channel_id=1, source_target_pairs={{2,3}} | collective-permute-start | bytes 3145736 | tf_op jit(solution)/shard_map/ppermute | solution.py:490
  11.6 2.4 %broadcast_select_fusion = f32[512,512]{1,0:T(8,128)} fusion(f32[512,512]{1,0:T(8,128)} %collective-permute-done.18, f32[512,512]{1,0:T(8,128)} %get-tuple-element.15.refs_11_, pred[]{:T(512)S(6)} %select_n.137), kind=kLoop, calls=%fused_computation.2 | loop fusion | flops 262144 | bytes 3145729 | tf_op jit(solution)/shard_map/jit(_where)/select_n | solution.py:546
  15.3 1.3 collective-permute-start.13
  16.6 3.0 %select_select_fusion = f32[512,512]{1,0:T(8,128)} fusion(f32[512,512]{1,0:T(8,128)} %collective-permute-done.1, f32[512,512]{1,0:T(8,128)} %collective-permute-done, f32[512,512]{1,0:T(8,128)S(1)} %collective-permute-done.2.refs_1_, f32[512,512]{1,0:T(8,128)S(1)} %copy-done.1, pred[]{:T(512)S(6)} %eq.15, pred[]{:T(512)S(6)} %eq.14, pred[]{:T(512)S(6)} %eq.13), kind=kLoop, calls=%fused_computation | loop fusion | flops 786432 | bytes 5242883 | tf_op jit(solution)/shard_map/jit(_where)/select_n | solution.py:588
  20.4 1.3 collective-permute-start.16
  21.7 8.7 %collective-permute-done.13.refs_4_ = f32[256,512]{1,0:T(8,128)} collective-permute-done((f32[256,512]{1,0:T(8,128)}, f32[256,512]{1,0:T(8,128)}, u32[]{:S(2)}, u32[]{:S(2)}) %collective-permute-start.13) | collective-permute-done | bytes 524320 | tf_op jit(solution)/shard_map/ppermute | solution.py:490
  30.4 1.9 %collective-permute-start.14 = (f32[256,512]{1,0:T(8,128)}, f32[256,512]{1,0:T(8,128)}, u32[]{:S(2)}, u32[]{:S(2)}) collective-permute-start(f32[256,512]{1,0:T(8,128)} %collective-permute-done.13.refs_4_), channel_id=1, source_target_pairs={{9,10},{13,14},{17,18},{21,22},{25,26},{29,30},{10,11},{14,15},{18... | collective-permute-start | bytes 1572872 | tf_op jit(solution)/shard_map/ppermute | solution.py:490
  33.4 2.0 %shard_map.42 = f32[264,512]{1,0:T(8,128)} custom-call(f32[512,512]{1,0:T(8,128)} %copy-done.9, f32[512,512]{1,0:T(8,128)} %get-tuple-element.11.own_ref.refs_0_), custom_call_target="tpu_custom_call" | custom-call | bytes 2637824 | tf_op jit(solution)/shard_map/pallas_call | solution.py:137
  36.3 3.4 %collective-permute-done.19 = f32[512,512]{1,0:T(8,128)} collective-permute-done((f32[512,512]{1,0:T(8,128)}, f32[512,512]{1,0:T(8,128)}, u32[]{:S(2)}, u32[]{:S(2)}) %collective-permute-start.19) | collective-permute-done | bytes 1048608 | tf_op jit(solution)/shard_map/ppermute | solution.py:490
  39.7 1.4 broadcast_select_fusion.1.refs_9_.refs_13_
  41.1 4.0 %collective-permute-start.20 = (f32[512,512]{1,0:T(8,128)S(1)}, f32[512,512]{1,0:T(8,128)S(1)}, u32[]{:S(2)}, u32[]{:S(2)}) collective-permute-start(f32[512,512]{1,0:T(8,128)S(1)} %broadcast_select_fusion.1.refs_9_.refs_13_), channel_id=1, source_target_pairs={{16,20},{20,16},{24,28},{28,24},{17,21},{21,17},{25,29},{29,25},{1... | collective-permute-start | bytes 3145736 | tf_op jit(solution)/shard_map/ppermute | solution.py:490
  45.1 2.9 %collective-permute-done.16.refs_7_ = f32[256,512]{1,0:T(8,128)} collective-permute-done((f32[256,512]{1,0:T(8,128)}, f32[256,512]{1,0:T(8,128)}, u32[]{:S(2)}, u32[]{:S(2)}) %collective-permute-start.16) | collective-permute-done | bytes 524320 | tf_op jit(solution)/shard_map/ppermute | solution.py:490
  48.7 10.5 %collective-permute-done.14.refs_5_ = f32[256,512]{1,0:T(8,128)} collective-permute-done((f32[256,512]{1,0:T(8,128)}, f32[256,512]{1,0:T(8,128)}, u32[]{:S(2)}, u32[]{:S(2)}) %collective-permute-start.14) | collective-permute-done | bytes 524320 | tf_op jit(solution)/shard_map/ppermute | solution.py:490
  60.0 1.9 %collective-permute-start.17 = (f32[256,512]{1,0:T(8,128)}, f32[256,512]{1,0:T(8,128)S(1)}, u32[]{:S(2)}, u32[]{:S(2)}) collective-permute-start(f32[256,512]{1,0:T(8,128)} %collective-permute-done.16.refs_7_), channel_id=1, source_target_pairs={{9,10},{13,14},{17,18},{21,22},{25,26},{29,30},{10,11},{14,15},{18... | collective-permute-start | bytes 1572872 | tf_op jit(solution)/shard_map/ppermute | solution.py:490
  61.9 1.3 collective-permute-start.15
  63.2 2.4 %broadcast_select_fusion.2 = f32[512,512]{1,0:T(8,128)} fusion(f32[512,512]{1,0:T(8,128)S(1)} %collective-permute-done.3.refs_10_, f32[512,512]{1,0:T(8,128)} %select_select_fusion, pred[]{:T(512)S(6)} %select_n.113), kind=kLoop, calls=%fused_computation.4 | loop fusion | flops 262144 | bytes 3145729 | tf_op jit(solution)/shard_map/jit(_where)/select_n | solution.py:546
  65.7 1.7 %collective-permute-start.4 = (f32[512,512]{1,0:T(8,128)}, f32[512,512]{1,0:T(8,128)}, u32[]{:S(2)}, u32[]{:S(2)}) collective-permute-start(f32[512,512]{1,0:T(8,128)} %broadcast_select_fusion.2), channel_id=1, source_target_pairs={{5,7},{0,16},{8,24},{1,17},{9,25},{2,18},{10,26},{3,19},{11,27}} | collective-permute-start | bytes 3145736 | tf_op jit(solution)/shard_map/ppermute | solution.py:490
  67.6 1.4 %collective-permute-start.10 = (f32[264,512]{1,0:T(8,128)S(1)}, f32[264,512]{1,0:T(8,128)}, u32[]{:S(2)}, u32[]{:S(2)}) collective-permute-start(f32[264,512]{1,0:T(8,128)S(1)} %select_select_fusion.1), channel_id=1, source_target_pairs={{4,20},{5,21},{6,22},{7,23}} | collective-permute-start | bytes 1622024 | tf_op jit(solution)/shard_map/ppermute | solution.py:490
  69.1 4.5 %collective-permute-done.17.refs_8_ = f32[256,512]{1,0:T(8,128)S(1)} collective-permute-done((f32[256,512]{1,0:T(8,128)}, f32[256,512]{1,0:T(8,128)S(1)}, u32[]{:S(2)}, u32[]{:S(2)}) %collective-permute-start.17) | collective-permute-done | bytes 524320 | tf_op jit(solution)/shard_map/ppermute | solution.py:490
  73.6 9.3 %collective-permute-done.15.refs_6_ = f32[256,512]{1,0:T(8,128)S(1)} collective-permute-done((f32[256,512]{1,0:T(8,128)}, f32[256,512]{1,0:T(8,128)S(1)}, u32[]{:S(2)}, u32[]{:S(2)}) %collective-permute-start.15) | collective-permute-done | bytes 524320 | tf_op jit(solution)/shard_map/ppermute | solution.py:490
  84.7 11.4 %shard_map.43 = (f32[1024,512]{1,0:T(8,128)}, f32[512,512]{1,0:T(8,128)}, f32[512,512]{1,0:T(8,128)}, f32[512,512]{1,0:T(8,128)}) custom-call(f32[512,512]{1,0:T(8,128)} %get-tuple-element.11.own_ref.refs_0_, f32[512,512]{1,0:T(8,128)} %copy-done.5, f32[512,512]{1,0:T(8,128)} %refs_9_.1, f32[512,512]{1,0:T(8,128)} %get-tuple-element.12.refs_3_.refs_6_, ...), custom_call_target="tpu_custom_call" | custom-call | flops 805306368 | bytes 15204352 | tf_op jit(solution)/shard_map/pallas_call | solution.py:137
  96.1 1.3 collective-permute-start.21
  98.6 1.3 collective-permute-start.11
  99.9 1.4 %broadcast_select_fusion.3.refs_2_ = f32[512,512]{1,0:T(8,128)S(1)} fusion(f32[512,512]{1,0:T(8,128)} %collective-permute-done.4.refs_11_, f32[512,512]{1,0:T(8,128)} %broadcast_select_fusion.2, pred[]{:T(512)S(6)} %select_n.111), kind=kLoop, calls=%fused_computation.5 | loop fusion | flops 262144 | bytes 3145729 | tf_op jit(solution)/shard_map/jit(_where)/select_n | solution.py:546
  102.6 6.1 %collective-permute-done.11 = f32[264,512]{1,0:T(8,128)} collective-permute-done((f32[264,512]{1,0:T(8,128)S(1)}, f32[264,512]{1,0:T(8,128)}, u32[]{:S(2)}, u32[]{:S(2)}) %collective-permute-start.11) | collective-permute-done | bytes 540704 | tf_op jit(solution)/shard_map/ppermute | solution.py:490
  109.9 1.3 collective-permute-start.12
  111.2 2.5 %collective-permute-start.22 = (f32[256,512]{1,0:T(8,128)}, f32[256,512]{1,0:T(8,128)S(1)}, u32[]{:S(2)}, u32[]{:S(2)}) collective-permute-start(f32[256,512]{1,0:T(8,128)} %copy-done.11), channel_id=1, source_target_pairs={{10,11},{14,15},{18,19},{22,23},{26,27},{30,31}} | collective-permute-start | bytes 1572872 | tf_op jit(solution)/shard_map/ppermute | solution.py:490
  113.8 8.8 %collective-permute-done.22.refs_8_ = f32[256,512]{1,0:T(8,128)S(1)} collective-permute-done((f32[256,512]{1,0:T(8,128)}, f32[256,512]{1,0:T(8,128)S(1)}, u32[]{:S(2)}, u32[]{:S(2)}) %collective-permute-start.22) | collective-permute-done | bytes 524320 | tf_op jit(solution)/shard_map/ppermute | solution.py:490
  124.4 19.1 %shard_map.44 = (f32[512,256]{1,0:T(8,128)}, f32[512,2,512]{2,1,0:T(2,128)}) custom-call(f32[512,512]{1,0:T(8,128)} %copy-done.8, f32[264,512]{1,0:T(8,128)} %copy-done.10, f32[512,512]{1,0:T(8,128)} %copy-done.4, f32[264,512]{1,0:T(8,128)} %copy-done.7, f32[1024,512]{1,0:T(8,128)} %get-tuple-element.16.refs_4_, ...), custom_call_target="tpu_custom_call" | custom-call | flops 1342177280 | bytes 19955712 | tf_op jit(solution)/shard_map/pallas_call | solution.py:137
  (54 shorter events, 14.0 us)
Async XLA Ops:
  5.0 11.6 %copy-start.1 = (f32[512,512]{1,0:T(8,128)S(1)}, f32[512,512]{1,0:T(8,128)}, u32[]{:S(2)}) copy-start(f32[512,512]{1,0:T(8,128)} %get-tuple-element.11.own_ref.refs_0_) | copy-start | bytes 3145732
  5.0 4.2 %collective-permute-start = (f32[512,512]{1,0:T(8,128)}, f32[512,512]{1,0:T(8,128)}, u32[]{:S(2)}, u32[]{:S(2)}) collective-permute-start(f32[512,512]{1,0:T(8,128)} %get-tuple-element.11.own_ref.refs_0_), channel_id=1, source_target_pairs={{1,2}} | collective-permute-start | bytes 3145736 | tf_op jit(solution)/shard_map/ppermute | solution.py:490
  6.8 4.8 %collective-permute-start.18 = (f32[512,512]{1,0:T(8,128)}, f32[512,512]{1,0:T(8,128)}, u32[]{:S(2)}, u32[]{:S(2)}) collective-permute-start(f32[512,512]{1,0:T(8,128)} %get-tuple-element.15.refs_11_), channel_id=1, source_target_pairs={{0,8},{1,9},{2,10},{3,11},{4,20},{5,21},{6,22},{7,23}} | collective-permute-start | bytes 3145736 | tf_op jit(solution)/shard_map/ppermute | solution.py:490
  8.4 8.1 %collective-permute-start.2 = (f32[512,512]{1,0:T(8,128)}, f32[512,512]{1,0:T(8,128)S(1)}, u32[]{:S(2)}, u32[]{:S(2)}) collective-permute-start(f32[512,512]{1,0:T(8,128)} %get-tuple-element.11.own_ref.refs_0_), channel_id=1, source_target_pairs={{1,0},{17,16},{21,20},{25,24},{29,28}} | collective-permute-start | bytes 3145736 | tf_op jit(solution)/shard_map/ppermute | solution.py:490
  9.2 7.4 %collective-permute-start.1 = (f32[512,512]{1,0:T(8,128)}, f32[512,512]{1,0:T(8,128)}, u32[]{:S(2)}, u32[]{:S(2)}) collective-permute-start(f32[512,512]{1,0:T(8,128)} %collective-permute-done), channel_id=1, source_target_pairs={{2,3}} | collective-permute-start | bytes 3145736 | tf_op jit(solution)/shard_map/ppermute | solution.py:490
  10.8 21.5 %collective-permute-start.6 = (f32[512,512]{1,0:T(8,128)}, f32[512,512]{1,0:T(8,128)S(1)}, u32[]{:S(2)}, u32[]{:S(2)}) collective-permute-start(f32[512,512]{1,0:T(8,128)} %get-tuple-element.11.own_ref.refs_0_), channel_id=1, source_target_pairs={{1,5}} | collective-permute-start | bytes 3145736 | tf_op jit(solution)/shard_map/ppermute | solution.py:490
  14.0 25.7 %collective-permute-start.19 = (f32[512,512]{1,0:T(8,128)}, f32[512,512]{1,0:T(8,128)}, u32[]{:S(2)}, u32[]{:S(2)}) collective-permute-start(f32[512,512]{1,0:T(8,128)} %broadcast_select_fusion), channel_id=1, source_target_pairs={{0,16},{8,24},{1,17},{9,25},{2,18},{10,26},{3,19},{11,27},{20,28},... | collective-permute-start | bytes 3145736 | tf_op jit(solution)/shard_map/ppermute | solution.py:490
  15.3 15.1 %collective-permute-start.13 = (f32[256,512]{1,0:T(8,128)}, f32[256,512]{1,0:T(8,128)}, u32[]{:S(2)}, u32[]{:S(2)}) collective-permute-start(f32[256,512]{1,0:T(8,128)} %get-tuple-element.13), channel_id=1, source_target_pairs={{0,1},{8,9},{12,13},{16,17},{20,21},{24,25},{28,29},{9,10},{13,14}... | collective-permute-start | bytes 1572872 | tf_op jit(solution)/shard_map/ppermute | solution.py:490
  16.6 3.1 %copy-start.5 = (f32[512,512]{1,0:T(8,128)}, f32[512,512]{1,0:T(8,128)S(1)}, u32[]{:S(2)}) copy-start(f32[512,512]{1,0:T(8,128)S(1)} %collective-permute-done.2.refs_1_) | copy-start | bytes 3145732
  19.7 42.2 %collective-permute-start.3 = (f32[512,512]{1,0:T(8,128)}, f32[512,512]{1,0:T(8,128)S(1)}, u32[]{:S(2)}, u32[]{:S(2)}) collective-permute-start(f32[512,512]{1,0:T(8,128)} %select_select_fusion), channel_id=1, source_target_pairs={{5,6},{0,8},{1,9},{2,10},{3,11}} | collective-permute-start | bytes 3145736 | tf_op jit(solution)/shard_map/ppermute | solution.py:490
  20.4 27.6 %collective-permute-start.16 = (f32[256,512]{1,0:T(8,128)}, f32[256,512]{1,0:T(8,128)}, u32[]{:S(2)}, u32[]{:S(2)}) collective-permute-start(f32[256,512]{1,0:T(8,128)} %get-tuple-element.14), channel_id=1, source_target_pairs={{0,1},{8,9},{12,13},{16,17},{20,21},{24,25},{28,29},{9,10},{13,14}... | collective-permute-start | bytes 1572872 | tf_op jit(solution)/shard_map/ppermute | solution.py:490
  30.4 28.8 %collective-permute-start.14 = (f32[256,512]{1,0:T(8,128)}, f32[256,512]{1,0:T(8,128)}, u32[]{:S(2)}, u32[]{:S(2)}) collective-permute-start(f32[256,512]{1,0:T(8,128)} %collective-permute-done.13.refs_4_), channel_id=1, source_target_pairs={{9,10},{13,14},{17,18},{21,22},{25,26},{29,30},{10,11},{14,15},{18... | collective-permute-start | bytes 1572872 | tf_op jit(solution)/shard_map/ppermute | solution.py:490
  35.4 12.6 %copy-start.6 = (f32[264,512]{1,0:T(8,128)S(1)}, f32[264,512]{1,0:T(8,128)}, u32[]{:S(2)}) copy-start(f32[264,512]{1,0:T(8,128)} %shard_map.42) | copy-start | bytes 1622020
  35.4 24.5 %collective-permute-start.9 = (f32[264,512]{1,0:T(8,128)}, f32[264,512]{1,0:T(8,128)S(1)}, u32[]{:S(2)}, u32[]{:S(2)}) collective-permute-start(f32[264,512]{1,0:T(8,128)} %shard_map.42), channel_id=1, source_target_pairs={{5,4}} | collective-permute-start | bytes 1622024 | tf_op jit(solution)/shard_map/ppermute | solution.py:490
  41.1 26.5 %copy-start = (f32[512,512]{1,0:T(8,128)}, f32[512,512]{1,0:T(8,128)S(1)}, u32[]{:S(2)}) copy-start(f32[512,512]{1,0:T(8,128)S(1)} %broadcast_select_fusion.1.refs_9_.refs_13_) | copy-start | bytes 3145732
  41.1 41.8 %collective-permute-start.20 = (f32[512,512]{1,0:T(8,128)S(1)}, f32[512,512]{1,0:T(8,128)S(1)}, u32[]{:S(2)}, u32[]{:S(2)}) collective-permute-start(f32[512,512]{1,0:T(8,128)S(1)} %broadcast_select_fusion.1.refs_9_.refs_13_), channel_id=1, source_target_pairs={{16,20},{20,16},{24,28},{28,24},{17,21},{21,17},{25,29},{29,25},{1... | collective-permute-start | bytes 3145736 | tf_op jit(solution)/shard_map/ppermute | solution.py:490
  48.0 17.6 %collective-permute-start.8 = (f32[264,512]{1,0:T(8,128)S(1)}, f32[264,512]{1,0:T(8,128)S(1)}, u32[]{:S(2)}, u32[]{:S(2)}) collective-permute-start(f32[264,512]{1,0:T(8,128)S(1)} %copy-done.6), channel_id=1, source_target_pairs={{5,6}} | collective-permute-start | bytes 1622024 | tf_op jit(solution)/shard_map/ppermute | solution.py:490
  59.3 8.1 %collective-permute-start.7 = (f32[264,512]{1,0:T(8,128)S(1)}, f32[264,512]{1,0:T(8,128)S(1)}, u32[]{:S(2)}, u32[]{:S(2)}) collective-permute-start(f32[264,512]{1,0:T(8,128)S(1)} %copy-done.6), channel_id=1, source_target_pairs={{5,7}} | collective-permute-start | bytes 1622024 | tf_op jit(solution)/shard_map/ppermute | solution.py:490
  60.0 13.6 %collective-permute-start.17 = (f32[256,512]{1,0:T(8,128)}, f32[256,512]{1,0:T(8,128)S(1)}, u32[]{:S(2)}, u32[]{:S(2)}) collective-permute-start(f32[256,512]{1,0:T(8,128)} %collective-permute-done.16.refs_7_), channel_id=1, source_target_pairs={{9,10},{13,14},{17,18},{21,22},{25,26},{29,30},{10,11},{14,15},{18... | collective-permute-start | bytes 1572872 | tf_op jit(solution)/shard_map/ppermute | solution.py:490
  61.9 5.7 %copy-start.3 = (f32[512,512]{1,0:T(8,128)}, f32[512,512]{1,0:T(8,128)S(1)}, u32[]{:S(2)}) copy-start(f32[512,512]{1,0:T(8,128)S(1)} %collective-permute-done.3.refs_10_) | copy-start | bytes 3145732
  61.9 21.0 %collective-permute-start.15 = (f32[256,512]{1,0:T(8,128)}, f32[256,512]{1,0:T(8,128)S(1)}, u32[]{:S(2)}, u32[]{:S(2)}) collective-permute-start(f32[256,512]{1,0:T(8,128)} %collective-permute-done.14.refs_5_), channel_id=1, source_target_pairs={{10,11},{14,15},{18,19},{22,23},{26,27},{30,31}} | collective-permute-start | bytes 1572872 | tf_op jit(solution)/shard_map/ppermute | solution.py:490
  65.7 34.2 %collective-permute-start.4 = (f32[512,512]{1,0:T(8,128)}, f32[512,512]{1,0:T(8,128)}, u32[]{:S(2)}, u32[]{:S(2)}) collective-permute-start(f32[512,512]{1,0:T(8,128)} %broadcast_select_fusion.2), channel_id=1, source_target_pairs={{5,7},{0,16},{8,24},{1,17},{9,25},{2,18},{10,26},{3,19},{11,27}} | collective-permute-start | bytes 3145736 | tf_op jit(solution)/shard_map/ppermute | solution.py:490
  67.6 29.8 %collective-permute-start.10 = (f32[264,512]{1,0:T(8,128)S(1)}, f32[264,512]{1,0:T(8,128)}, u32[]{:S(2)}, u32[]{:S(2)}) collective-permute-start(f32[264,512]{1,0:T(8,128)S(1)} %select_select_fusion.1), channel_id=1, source_target_pairs={{4,20},{5,21},{6,22},{7,23}} | collective-permute-start | bytes 1622024 | tf_op jit(solution)/shard_map/ppermute | solution.py:490
  73.6 10.1 %copy-start.11 = (f32[256,512]{1,0:T(8,128)}, f32[256,512]{1,0:T(8,128)S(1)}, u32[]{:S(2)}) copy-start(f32[256,512]{1,0:T(8,128)S(1)} %collective-permute-done.17.refs_8_) | copy-start | bytes 1572868
  83.7 1.0 copy-start.2
  96.1 27.3 %collective-permute-start.21 = (f32[1024,512]{1,0:T(8,128)}, f32[1024,512]{1,0:T(8,128)}, u32[]{:S(2)}, u32[]{:S(2)}) collective-permute-start(f32[1024,512]{1,0:T(8,128)} %get-tuple-element.16.refs_4_), channel_id=1, source_target_pairs={{26,30}} | collective-permute-start | bytes 6291464 | tf_op jit(solution)/shard_map/ppermute | solution.py:490
  98.6 10.2 %collective-permute-start.11 = (f32[264,512]{1,0:T(8,128)S(1)}, f32[264,512]{1,0:T(8,128)}, u32[]{:S(2)}, u32[]{:S(2)}) collective-permute-start(f32[264,512]{1,0:T(8,128)S(1)} %broadcast_select_fusion.4), channel_id=1, source_target_pairs={{4,12},{20,28},{5,13},{21,29},{6,14},{22,30},{7,15},{23,31}} | collective-permute-start | bytes 1622024 | tf_op jit(solution)/shard_map/ppermute | solution.py:490
  101.3 22.1 %copy-start.4 = (f32[512,512]{1,0:T(8,128)}, f32[512,512]{1,0:T(8,128)S(1)}, u32[]{:S(2)}) copy-start(f32[512,512]{1,0:T(8,128)S(1)} %broadcast_select_fusion.3.refs_2_) | copy-start | bytes 3145732
  101.3 21.2 %collective-permute-start.5 = (f32[512,512]{1,0:T(8,128)S(1)}, f32[512,512]{1,0:T(8,128)S(1)}, u32[]{:S(2)}, u32[]{:S(2)}) collective-permute-start(f32[512,512]{1,0:T(8,128)S(1)} %broadcast_select_fusion.3.refs_2_), channel_id=1, source_target_pairs={{0,4},{8,12},{16,20},{24,28},{1,5},{9,13},{17,21},{25,29},{2,6},{1... | collective-permute-start | bytes 3145736 | tf_op jit(solution)/shard_map/ppermute | solution.py:490
  109.9 13.5 %copy-start.7 = (f32[264,512]{1,0:T(8,128)}, f32[264,512]{1,0:T(8,128)S(1)}, u32[]{:S(2)}) copy-start(f32[264,512]{1,0:T(8,128)S(1)} %broadcast_select_fusion.5.refs_3_) | copy-start | bytes 1622020
  109.9 12.7 %collective-permute-start.12 = (f32[264,512]{1,0:T(8,128)S(1)}, f32[264,512]{1,0:T(8,128)S(1)}, u32[]{:S(2)}, u32[]{:S(2)}) collective-permute-start(f32[264,512]{1,0:T(8,128)S(1)} %broadcast_select_fusion.5.refs_3_), channel_id=1, source_target_pairs={{4,0},{12,8},{20,16},{28,24},{5,1},{13,9},{21,17},{29,25},{6,2},{1... | collective-permute-start | bytes 1622024 | tf_op jit(solution)/shard_map/ppermute | solution.py:490
  111.2 11.3 %collective-permute-start.22 = (f32[256,512]{1,0:T(8,128)}, f32[256,512]{1,0:T(8,128)S(1)}, u32[]{:S(2)}, u32[]{:S(2)}) collective-permute-start(f32[256,512]{1,0:T(8,128)} %copy-done.11), channel_id=1, source_target_pairs={{10,11},{14,15},{18,19},{22,23},{26,27},{30,31}} | collective-permute-start | bytes 1572872 | tf_op jit(solution)/shard_map/ppermute | solution.py:490
  (5 other events, 4.6 us)

commit v2 on v1

--- a/solution.py
+++ b/solution.py
@@ -163,6 +163,33 @@
     return groups
 
 
+def pick(choices, kept=None):
+    count, shape = len(choices), choices[0][1].shape
+
+    def kernel(*refs):
+        out_ref, buffer, sems = refs[count:]
+        r, c = place()
+        for k, ((condition, _), source) in enumerate(zip(choices, refs[:count])):
+            if k == kept:
+                continue
+
+            @pl.when(condition(r, c))
+            def _(source=source):
+                for i, (a, b) in enumerate(((source, buffer), (buffer, out_ref))):
+                    copy = pltpu.make_async_copy(a, b, sems.at[i])
+                    copy.start()
+                    copy.wait()
+
+    return pl.pallas_call(
+        kernel,
+        out_shape=jax.ShapeDtypeStruct(shape, jnp.float32),
+        in_specs=[pl.BlockSpec(memory_space=pltpu.HBM)] * count,
+        out_specs=pl.BlockSpec(memory_space=pltpu.HBM),
+        scratch_shapes=[vmem(*shape), copies(2)],
+        input_output_aliases={} if kept is None else {kept: 0},
+    )(*[array for _, array in choices])
+
+
 def extract_kernel(cov_ref, diag_ref, lead_ref, low_ref, high_ref, *refs):
     held_refs, dinv, sems = refs[:-2], refs[-2], refs[-1]
     half = low_ref.shape[0]
@@ -336,6 +363,7 @@
     own = (c >= 2) & (r == last)
     near = (c >= 2) & (r == last + 1) & (r // 2 == last // 2)
     late = c == cols - 1
+    which = jnp.where(own, 0, 1)
 
     def wanted(t):
         found = r >= (t + jnp.where(c < 2, 1, 0)) * cols + c
@@ -383,16 +411,9 @@
     def _():
         pltpu.make_async_copy(near_pair, near_stack, sems.at[1]).wait()
 
-    @pl.when(own | near)
-    def _():
-        pltpu.make_async_copy(held, near_total, sems.at[2]).wait()
-
     @pl.when(jnp.logical_not(late))
     def _():
         pltpu.make_async_copy(pair, stack, sems.at[0]).wait()
-
-    for wait in waits:
-        wait()
 
     @pl.when(late)
     def _():
@@ -401,11 +422,6 @@
         pltpu.make_async_copy(pair.at[bottom], stack.at[bottom], sems.at[4]).wait()
         pltpu.make_async_copy(last_rows, stack.at[high], sems.at[5]).wait()
         stack[high, :] = nt(stack[high, :], near_stack[top, :])
-        for t in range(tiles):
-
-            @pl.when(wanted(t))
-            def _(t=t):
-                total[t, high] = total[t, high] - nn(stack[high, :], first[t])
 
     @pl.when(r == 1)
     def _():
@@ -444,6 +460,8 @@
             panels_ref[...] = stack[rows, start : start + width]
 
     trailing_ref[...] = jnp.zeros_like(trailing_ref)
+    for wait in waits:
+        wait()
 
     def store(t, value):
         for shift in (0, 1):
@@ -457,23 +475,27 @@
 
         @pl.when(wanted(t))
         def _(t=t):
+            @pl.when(late)
+            def _():
+                total[t, high] = total[t, high] - nn(stack[high, :], first[t])
+
             second[t] = second[t] - tn(corner[...], first[t])
             upper, lower = second[t, low], second[t, high]
             second[t, low] = dot3(g_first, upper, 1, 0)
             second[t, high] = dot3(g_below, upper, 1, 0) + dot3(g_second_t, lower, 0, 0)
             store(t, total[t] - dot3(stack[bottom, :], second[t], 1, 0))
 
-    @pl.when(own)
-    def _():
-        near_stack[...] = stack[...]
+    @pl.when(own | near)
+    def _():
+        pltpu.make_async_copy(held, near_total, sems.at[2]).wait()
 
     @pl.when(near | (own & late))
     def _():
-        near_total[...] = near_total[...] - nt(stack[top, :], near_stack[top, :])
+        near_total[...] = near_total[...] - nt(stack[top, :], stacks[which, top])
 
     @pl.when(own | near)
     def _():
-        store(cycles - 1, near_total[...] - dot3(stack[bottom, :], near_stack[bottom, :], 1, 1))
+        store(cycles - 1, near_total[...] - dot3(stack[bottom, :], stacks[which, bottom], 1, 1))
 
 
 def local(covariance, diag_inverse, rows, cols):
@@ -481,7 +503,7 @@
     cycles = covariance.shape[1]
     half = tile // 2
     chips = rows // 2
-    r, c = place()
+    r, _ = place()
     chip, core = r // 2, r % 2
     whole = (tile, tile)
 
@@ -524,15 +546,15 @@
         moved.append(chain)
     back = send(lead, [((a, 1), (a, 0)) for a in range(rows) if a == 0 or a >= min(cols, rows - 1)])
 
-    def spread(value, wanted, cores, extra=()):
-        current, arrivals = value, []
+    def spread(value, wanted, cores, kept=1):
+        current = value
         for step in range(len(bits)):
-            pairs = list(extra[step : step + 1])
-            arrived = False
+            pairs, arrived, seen = [], False, {}
             for k in cores:
                 order = bits if k == 0 else bits[::-1]
                 used, bit, later = sum(order[:step]), order[step], sum(order[step + 1 :])
                 arrived = jnp.where(core == k, (chip & bit) != 0, arrived)
+                seen[k] = (used | bit, bit)
                 for column in range(cols):
                     for q in range(chips):
                         target = q | bit
@@ -541,10 +563,28 @@
                         reach = {target | more for more in range(chips) if not more & ~later}
                         if reach & wanted(column):
                             pairs.append(((2 * q + k, column), (2 * target + k, column)))
-            if pairs:
-                arrivals.append(send(current, pairs))
-                current = jnp.where(arrived, arrivals[-1], current)
-        return current, arrivals
+            if not pairs:
+                continue
+            got = send(current, pairs)
+            if step + 1 == len(bits):
+                current = jnp.where(arrived, got, current)
+                continue
+
+            def holds(r, c, new, seen=seen):
+                found = False
+                for k, (inside, bit) in seen.items():
+                    at = (r % 2 == k) & ((r // 2 & ~inside) == 0)
+                    found = found | (at & (((r // 2 & bit) != 0) == new))
+                return found
+
+            current = pick(
+                [
+                    (functools.partial(holds, new=True), got),
+                    (functools.partial(holds, new=False), current),
+                ],
+                kept if step == 0 else 1,
+            )
+        return current
 
     def trade(value, wanted, ways=(0, 1)):
         pairs = []
@@ -563,7 +603,7 @@
             return {q for q in range(chips) if q >= edge and q > 0}
 
         if any(wanted(column) for column in range(cols)):
-            mine.append(spread(held[t], wanted, (0, 1))[0])
+            mine.append(spread(held[t], wanted, (0, 1), kept=None))
             other.append(trade(mine[-1], wanted))
     tiles = len(mine)
 
@@ -582,19 +622,28 @@
     def everyone(column):
         return set(range(chips))
 
-    corner, passed = jnp.where(c == 0, back, lead), lead
+    choices = [
+        (lambda r, c: (r == 0) & (c == 0), back),
+        (lambda r, c: (r == 0) & (c == 1), lead),
+    ]
     for b in range(2, cols):
-        passed = send(passed, [((0, b - 1), (0, b))])
-        corner = jnp.where(c == b, passed, corner)
-    extra = [((1, 1), (1, b)) for b in range(cols // 2, cols)]
-    corner, arrivals = spread(corner, everyone, (0,), extra)
+        array = send(lead, [((0, 1), (0, b))])
+        choices.append((lambda r, c, b=b: (r == 0) & (c == b), array))
+    corner = pick(choices)
+    corner = spread(corner, everyone, (0,))
+
+    passed = []
+    for b in range(cols // 2, cols):
+        passed.append(send(lead, [((1, 1), (1, b))]))
     corner_odd = trade(corner, everyone, (0,))
 
-    piece = packed
+    choices = [(lambda r, c: (r == 1) & (c == 1), packed)]
     for b in range(cols):
         if b != 1:
-            piece = jnp.where(c == b, send(packed, [((1, 1), (1, b))]), piece)
-    piece_odd, _ = spread(piece, everyone, (1,))
+            array = send(packed, [((1, 1), (1, b))])
+            choices.append((lambda r, c, b=b: (r == 1) & (c == b), array))
+    piece = pick(choices, 0)
+    piece_odd = spread(piece, everyone, (1,))
     piece_even = trade(piece_odd, everyone, (1,))
 
     product = 2 * tile**3
@@ -612,13 +661,12 @@
     edges = [column_of(cycles - 1, b) for b in range(2, cols)]
     pairs = [((j, b), (j + 1, b)) for b, j in zip(range(2, cols), edges) if j % 2 == 0]
     near_pair = send(pair, pairs)
-    rows_of_one = cols // 2
     panels, trailing = call(
         functools.partial(final_kernel, cols, cycles, tiles),
         [(tile, 2 * tile // cols), covariance.shape],
         [
             corner_odd, piece_even, corner, piece_odd, pair, near_pair, held[-1], near_part,
-            moved[1][-1], diag_inverse, *arrivals[:rows_of_one],
+            moved[1][-1], diag_inverse, *passed,
             *first_t, *mine, *other, *partial,
         ],
         [vmem(half + SUB, tile), vmem(*whole), vmem(2, 2 * tile, tile)]

time: 145 us -> 141 us (0.972)
  other arithmetic: 13.2 us -> 2.72 us
  starting transfers between devices: 33.3 us -> 40 us
  waiting for transfers between devices: 54.4 us -> 57.1 us
  local copies, waits for them, and re-layouts: 4.59 us -> 2.88 us
    select_n x8 -> x3, other arithmetic: 13.2 us -> 2.72 us  [spread(): current = jnp.where(arrived, got, current)]
    ppermute x23 -> x25, starting transfers between devices: 33.3 us -> 40 us  [send(): return lax.ppermute(value, AXES, flat)]
    ppermute x23 -> x25, waiting for transfers between devices: 54.4 us -> 57.1 us  [send(): return lax.ppermute(value, AXES, flat)]
    unnamed x28 -> x24, local copies, waits for them, and re-layouts: 4.59 us -> 2.88 us
  transfers between devices with their start and end apart: 23 -> 25, of which waited for: 8 -> 7; matrix products, arithmetic and copies ran while one was open for 9% -> 2% of each run, Pallas kernels for 9% -> 10%
where the time goes in v2:
time: 141 us
  waiting for transfers between devices  57.1 us (40%)
  starting transfers between devices  40 us (28%)
  Pallas kernels  36.8 us (26%)
  local copies, waits for them, and re-layouts  2.88 us (2%)
  other arithmetic  2.72 us (2%)
    ppermute x25, waiting for transfers between devices, send(): return lax.ppermute(value, AXES, flat)  57.1 us
    ppermute x25, starting transfers between devices, send(): return lax.ppermute(value, AXES, flat)  40 us
    pallas_call x4, Pallas kernels, call(): pl.pallas_call(kernel, out_shape=outs, in_specs=[pl.BlockSpec(memory_spac...  36.6 us
    unnamed x24, local copies, waits for them, and re-layouts  2.88 us
  transfers between devices with their start and end apart: 25, of which 7 were waited for; matrix products, arithmetic and copies ran while one was open for 2% of the time, Pallas kernels for 10%

profile of v2, /device:TPU:23, one launch (start us, length us, event | category | flops | bytes accessed | tf_op | source)
XLA Modules:
  0.0 140.6 jit_solution(14315710023224813081)
XLA Ops:
  0.6 4.3 %shard_map.41 = (f32[512,512]{1,0:T(8,128)}, f32[256,512]{1,0:T(8,128)}, f32[256,512]{1,0:T(8,128)}, f32[512,512]{1,0:T(8,128)}, f32[512,512]{1,0:T(8,128)}) custom-call(f32[512,2,512]{2,1,0:T(2,128)} %cov_ref.1, f32[512,512]{1,0:T(8,128)} %refs_9_.1), custom_call_target="tpu_custom_call" | custom-call | bytes 7340032 | tf_op jit(solution)/shard_map/pallas_call | solution.py:137
  5.0 1.8 %collective-permute-start.18 = (f32[512,512]{1,0:T(8,128)}, f32[512,512]{1,0:T(8,128)}, u32[]{:S(2)}, u32[]{:S(2)}) collective-permute-start(f32[512,512]{1,0:T(8,128)} %get-tuple-element.15.refs_1_.refs_11_), channel_id=1, source_target_pairs={{0,8},{1,9},{2,10},{3,11},{4,20},{5,21},{6,22},{7,23}} | collective-permute-start | bytes 3145736 | tf_op jit(solution)/shard_map/ppermute | solution.py:512
  8.2 1.7 %collective-permute-start.2 = (f32[512,512]{1,0:T(8,128)}, f32[512,512]{1,0:T(8,128)}, u32[]{:S(2)}, u32[]{:S(2)}) collective-permute-start(f32[512,512]{1,0:T(8,128)} %get-tuple-element.11.refs_1_.own_ref.refs_0_), channel_id=1, source_target_pairs={{1,3}} | collective-permute-start | bytes 3145736 | tf_op jit(solution)/shard_map/ppermute | solution.py:512
  9.9 1.3 collective-permute-start.19
  11.2 1.3 collective-permute-start.13
  12.5 13.8 %collective-permute-done.13.refs_4_ = f32[256,512]{1,0:T(8,128)} collective-permute-done((f32[256,512]{1,0:T(8,128)}, f32[256,512]{1,0:T(8,128)}, u32[]{:S(2)}, u32[]{:S(2)}) %collective-permute-start.13) | collective-permute-done | bytes 524320 | tf_op jit(solution)/shard_map/ppermute | solution.py:512
  26.3 1.7 %collective-permute-start.6 = (f32[512,512]{1,0:T(8,128)S(1)}, f32[512,512]{1,0:T(8,128)}, u32[]{:S(2)}, u32[]{:S(2)}) collective-permute-start(f32[512,512]{1,0:T(8,128)S(1)} %copy-done), channel_id=1, source_target_pairs={{1,5}} | collective-permute-start | bytes 3145736 | tf_op jit(solution)/shard_map/ppermute | solution.py:512
  28.0 1.3 collective-permute-start.16
  29.3 1.9 %collective-permute-start.14 = (f32[256,512]{1,0:T(8,128)}, f32[256,512]{1,0:T(8,128)}, u32[]{:S(2)}, u32[]{:S(2)}) collective-permute-start(f32[256,512]{1,0:T(8,128)} %collective-permute-done.13.refs_4_), channel_id=1, source_target_pairs={{9,10},{13,14},{17,18},{21,22},{25,26},{29,30},{10,11},{14,15},{18... | collective-permute-start | bytes 1572872 | tf_op jit(solution)/shard_map/ppermute | solution.py:512
  31.3 1.7 %collective-permute-start.3 = (f32[512,512]{1,0:T(8,128)}, f32[512,512]{1,0:T(8,128)}, u32[]{:S(2)}, u32[]{:S(2)}) collective-permute-start(f32[512,512]{1,0:T(8,128)} %shard_map.42.refs_1_), channel_id=1, source_target_pairs={{0,8},{1,9},{2,10},{3,11}} | collective-permute-start | bytes 3145736 | tf_op jit(solution)/shard_map/ppermute | solution.py:512
  33.0 4.8 %collective-permute-done.19 = f32[512,512]{1,0:T(8,128)} collective-permute-done((f32[512,512]{1,0:T(8,128)}, f32[512,512]{1,0:T(8,128)}, u32[]{:S(2)}, u32[]{:S(2)}) %collective-permute-start.19) | collective-permute-done | bytes 1048608 | tf_op jit(solution)/shard_map/ppermute | solution.py:512
  37.8 1.4 %broadcast_select_fusion.refs_9_.refs_13_ = f32[512,512]{1,0:T(8,128)S(1)} fusion(f32[512,512]{1,0:T(8,128)} %collective-permute-done.19, f32[512,512]{1,0:T(8,128)} %shard_map.47, pred[]{:T(512)S(6)} %select_n.53), kind=kLoop, calls=%fused_computation | loop fusion | flops 262144 | bytes 3145729 | tf_op jit(solution)/shard_map/jit(_where)/select_n | solution.py:570
  39.2 4.0 %collective-permute-start.20 = (f32[512,512]{1,0:T(8,128)S(1)}, f32[512,512]{1,0:T(8,128)S(1)}, u32[]{:S(2)}, u32[]{:S(2)}) collective-permute-start(f32[512,512]{1,0:T(8,128)S(1)} %broadcast_select_fusion.refs_9_.refs_13_), channel_id=1, source_target_pairs={{16,20},{20,16},{24,28},{28,24},{17,21},{21,17},{25,29},{29,25},{1... | collective-permute-start | bytes 3145736 | tf_op jit(solution)/shard_map/ppermute | solution.py:512
  44.1 2.4 %collective-permute-start.17 = (f32[256,512]{1,0:T(8,128)}, f32[256,512]{1,0:T(8,128)}, u32[]{:S(2)}, u32[]{:S(2)}) collective-permute-start(f32[256,512]{1,0:T(8,128)} %collective-permute-done.16.refs_7_), channel_id=1, source_target_pairs={{9,10},{13,14},{17,18},{21,22},{25,26},{29,30},{10,11},{14,15},{18... | collective-permute-start | bytes 1572872 | tf_op jit(solution)/shard_map/ppermute | solution.py:512
  46.5 8.9 %collective-permute-done.14.refs_5_ = f32[256,512]{1,0:T(8,128)} collective-permute-done((f32[256,512]{1,0:T(8,128)}, f32[256,512]{1,0:T(8,128)}, u32[]{:S(2)}, u32[]{:S(2)}) %collective-permute-start.14) | collective-permute-done | bytes 524320 | tf_op jit(solution)/shard_map/ppermute | solution.py:512
  55.3 2.1 %collective-permute-start.15 = (f32[256,512]{1,0:T(8,128)}, f32[256,512]{1,0:T(8,128)}, u32[]{:S(2)}, u32[]{:S(2)}) collective-permute-start(f32[256,512]{1,0:T(8,128)} %collective-permute-done.14.refs_5_), channel_id=1, source_target_pairs={{10,11},{14,15},{18,19},{22,23},{26,27},{30,31}} | collective-permute-start | bytes 1572872 | tf_op jit(solution)/shard_map/ppermute | solution.py:512
  57.4 2.1 %shard_map.44.refs_0_ = f32[264,512]{1,0:T(8,128)} custom-call(f32[512,512]{1,0:T(8,128)} %collective-permute-done.6.corner_ref, f32[512,512]{1,0:T(8,128)} %get-tuple-element.11.refs_1_.own_ref.refs_0_), custom_call_target="tpu_custom_call" | custom-call | bytes 2637824 | tf_op jit(solution)/shard_map/pallas_call | solution.py:137
  59.5 1.5 %collective-permute-start.7 = (f32[264,512]{1,0:T(8,128)}, f32[264,512]{1,0:T(8,128)}, u32[]{:S(2)}, u32[]{:S(2)}) collective-permute-start(f32[264,512]{1,0:T(8,128)} %shard_map.44.refs_0_), channel_id=1, source_target_pairs={{5,4}} | collective-permute-start | bytes 1622024 | tf_op jit(solution)/shard_map/ppermute | solution.py:512
  60.9 5.6 %collective-permute-done.17.refs_8_ = f32[256,512]{1,0:T(8,128)} collective-permute-done((f32[256,512]{1,0:T(8,128)}, f32[256,512]{1,0:T(8,128)}, u32[]{:S(2)}, u32[]{:S(2)}) %collective-permute-start.17) | collective-permute-done | bytes 524320 | tf_op jit(solution)/shard_map/ppermute | solution.py:512
  66.6 1.5 %collective-permute-start.8 = (f32[264,512]{1,0:T(8,128)}, f32[264,512]{1,0:T(8,128)}, u32[]{:S(2)}, u32[]{:S(2)}) collective-permute-start(f32[264,512]{1,0:T(8,128)} %shard_map.44.refs_0_), channel_id=1, source_target_pairs={{5,6}} | collective-permute-start | bytes 1622024 | tf_op jit(solution)/shard_map/ppermute | solution.py:512
  68.0 1.5 %collective-permute-start.9 = (f32[264,512]{1,0:T(8,128)}, f32[264,512]{1,0:T(8,128)}, u32[]{:S(2)}, u32[]{:S(2)}) collective-permute-start(f32[264,512]{1,0:T(8,128)} %shard_map.44.refs_0_), channel_id=1, source_target_pairs={{5,7}} | collective-permute-start | bytes 1622024 | tf_op jit(solution)/shard_map/ppermute | solution.py:512
  69.6 1.7 %collective-permute-start.4 = (f32[512,512]{1,0:T(8,128)}, f32[512,512]{1,0:T(8,128)}, u32[]{:S(2)}, u32[]{:S(2)}) collective-permute-start(f32[512,512]{1,0:T(8,128)} %shard_map.43), channel_id=1, source_target_pairs={{0,16},{8,24},{1,17},{9,25},{2,18},{10,26},{3,19},{11,27}} | collective-permute-start | bytes 3145736 | tf_op jit(solution)/shard_map/ppermute | solution.py:512
  72.3 11.2 %shard_map.48 = (f32[1024,512]{1,0:T(8,128)}, f32[512,512]{1,0:T(8,128)}, f32[512,512]{1,0:T(8,128)}, f32[512,512]{1,0:T(8,128)}) custom-call(f32[512,512]{1,0:T(8,128)} %get-tuple-element.11.refs_1_.own_ref.refs_0_, f32[512,512]{1,0:T(8,128)} %copy-done.5, f32[512,512]{1,0:T(8,128)} %refs_9_.1, f32[512,512]{1,0:T(8,128)} %get-tuple-element.12.refs_3_.refs_6_, ...), custom_call_target="tpu_custom_call" | custom-call | flops 805306368 | bytes 15204352 | tf_op jit(solution)/shard_map/pallas_call | solution.py:137
  83.5 1.4 %collective-permute-start.21 = (f32[1024,512]{1,0:T(8,128)}, f32[1024,512]{1,0:T(8,128)}, u32[]{:S(2)}, u32[]{:S(2)}) collective-permute-start(f32[1024,512]{1,0:T(8,128)} %get-tuple-element.16.refs_4_), channel_id=1, source_target_pairs={{26,30}} | collective-permute-start | bytes 6291464 | tf_op jit(solution)/shard_map/ppermute | solution.py:512
  85.7 1.6 %collective-permute-start.23 = (f32[512,512]{1,0:T(8,128)S(1)}, f32[512,512]{1,0:T(8,128)}, u32[]{:S(2)}, u32[]{:S(2)}) collective-permute-start(f32[512,512]{1,0:T(8,128)S(1)} %copy-done.1), channel_id=1, source_target_pairs={{5,6}} | collective-permute-start | bytes 3145736 | tf_op jit(solution)/shard_map/ppermute | solution.py:512
  87.4 1.6 %collective-permute-start.24 = (f32[512,512]{1,0:T(8,128)S(1)}, f32[512,512]{1,0:T(8,128)}, u32[]{:S(2)}, u32[]{:S(2)}) collective-permute-start(f32[512,512]{1,0:T(8,128)S(1)} %copy-done.1), channel_id=1, source_target_pairs={{5,7}} | collective-permute-start | bytes 3145736 | tf_op jit(solution)/shard_map/ppermute | solution.py:512
  89.9 1.4 %collective-permute-start.11 = (f32[264,512]{1,0:T(8,128)}, f32[264,512]{1,0:T(8,128)S(1)}, u32[]{:S(2)}, u32[]{:S(2)}) collective-permute-start(f32[264,512]{1,0:T(8,128)} %shard_map.46), channel_id=1, source_target_pairs={{4,12},{20,28},{5,13},{21,29},{6,14},{22,30},{7,15},{23,31}} | collective-permute-start | bytes 1622024 | tf_op jit(solution)/shard_map/ppermute | solution.py:512
  93.8 16.7 %collective-permute-done.11 = f32[264,512]{1,0:T(8,128)S(1)} collective-permute-done((f32[264,512]{1,0:T(8,128)}, f32[264,512]{1,0:T(8,128)S(1)}, u32[]{:S(2)}, u32[]{:S(2)}) %collective-permute-start.11) | collective-permute-done | bytes 540704 | tf_op jit(solution)/shard_map/ppermute | solution.py:512
  110.6 1.3 collective-permute-start.12
  111.9 2.1 %collective-permute-start.22 = (f32[256,512]{1,0:T(8,128)}, f32[256,512]{1,0:T(8,128)S(1)}, u32[]{:S(2)}, u32[]{:S(2)}) collective-permute-start(f32[256,512]{1,0:T(8,128)} %collective-permute-done.17.refs_8_), channel_id=1, source_target_pairs={{10,11},{14,15},{18,19},{22,23},{26,27},{30,31}} | collective-permute-start | bytes 1572872 | tf_op jit(solution)/shard_map/ppermute | solution.py:512
  114.0 6.4 %collective-permute-done.22.refs_8_ = f32[256,512]{1,0:T(8,128)S(1)} collective-permute-done((f32[256,512]{1,0:T(8,128)}, f32[256,512]{1,0:T(8,128)S(1)}, u32[]{:S(2)}, u32[]{:S(2)}) %collective-permute-start.22) | collective-permute-done | bytes 524320 | tf_op jit(solution)/shard_map/ppermute | solution.py:512
  121.4 19.1 %shard_map.49 = (f32[512,256]{1,0:T(8,128)}, f32[512,2,512]{2,1,0:T(2,128)}) custom-call(f32[512,512]{1,0:T(8,128)} %collective-permute-done.5.refs_0_, f32[264,512]{1,0:T(8,128)} %copy-done.10, f32[512,512]{1,0:T(8,128)} %broadcast_select_fusion.1.refs_2_, f32[264,512]{1,0:T(8,128)} %copy-done.7, f32[1024,512]{1,0:T(8,128)} %get-tuple-element.16.refs_4_, ...), custom_call_target="tpu_custom_call" | custom-call | flops 1342177280 | bytes 19955712 | tf_op jit(solution)/shard_map/pallas_call | solution.py:137
  (54 shorter events, 8.6 us)
Async XLA Ops:
  4.9 21.4 %copy-start = (f32[512,512]{1,0:T(8,128)S(1)}, f32[512,512]{1,0:T(8,128)}, u32[]{:S(2)}) copy-start(f32[512,512]{1,0:T(8,128)} %get-tuple-element.11.refs_1_.own_ref.refs_0_) | copy-start | bytes 3145732
  5.0 4.9 %collective-permute-start.18 = (f32[512,512]{1,0:T(8,128)}, f32[512,512]{1,0:T(8,128)}, u32[]{:S(2)}, u32[]{:S(2)}) collective-permute-start(f32[512,512]{1,0:T(8,128)} %get-tuple-element.15.refs_1_.refs_11_), channel_id=1, source_target_pairs={{0,8},{1,9},{2,10},{3,11},{4,20},{5,21},{6,22},{7,23}} | collective-permute-start | bytes 3145736 | tf_op jit(solution)/shard_map/ppermute | solution.py:512
  6.7 21.3 %collective-permute-start = (f32[512,512]{1,0:T(8,128)}, f32[512,512]{1,0:T(8,128)S(1)}, u32[]{:S(2)}, u32[]{:S(2)}) collective-permute-start(f32[512,512]{1,0:T(8,128)} %get-tuple-element.11.refs_1_.own_ref.refs_0_), channel_id=1, source_target_pairs={{1,0},{17,16},{21,20},{25,24},{29,28}} | collective-permute-start | bytes 3145736 | tf_op jit(solution)/shard_map/ppermute | solution.py:512
  7.5 21.8 %collective-permute-start.1 = (f32[512,512]{1,0:T(8,128)}, f32[512,512]{1,0:T(8,128)S(1)}, u32[]{:S(2)}, u32[]{:S(2)}) collective-permute-start(f32[512,512]{1,0:T(8,128)} %get-tuple-element.11.refs_1_.own_ref.refs_0_), channel_id=1, source_target_pairs={{1,2}} | collective-permute-start | bytes 3145736 | tf_op jit(solution)/shard_map/ppermute | solution.py:512
  8.2 23.1 %collective-permute-start.2 = (f32[512,512]{1,0:T(8,128)}, f32[512,512]{1,0:T(8,128)}, u32[]{:S(2)}, u32[]{:S(2)}) collective-permute-start(f32[512,512]{1,0:T(8,128)} %get-tuple-element.11.refs_1_.own_ref.refs_0_), channel_id=1, source_target_pairs={{1,3}} | collective-permute-start | bytes 3145736 | tf_op jit(solution)/shard_map/ppermute | solution.py:512
  9.9 27.9 %collective-permute-start.19 = (f32[512,512]{1,0:T(8,128)}, f32[512,512]{1,0:T(8,128)}, u32[]{:S(2)}, u32[]{:S(2)}) collective-permute-start(f32[512,512]{1,0:T(8,128)} %shard_map.47), channel_id=1, source_target_pairs={{0,16},{8,24},{1,17},{9,25},{2,18},{10,26},{3,19},{11,27},{20,28},... | collective-permute-start | bytes 3145736 | tf_op jit(solution)/shard_map/ppermute | solution.py:512
  11.2 15.1 %collective-permute-start.13 = (f32[256,512]{1,0:T(8,128)}, f32[256,512]{1,0:T(8,128)}, u32[]{:S(2)}, u32[]{:S(2)}) collective-permute-start(f32[256,512]{1,0:T(8,128)} %get-tuple-element.13), channel_id=1, source_target_pairs={{0,1},{8,9},{12,13},{16,17},{20,21},{24,25},{28,29},{9,10},{13,14}... | collective-permute-start | bytes 1572872 | tf_op jit(solution)/shard_map/ppermute | solution.py:512
  26.3 31.1 %collective-permute-start.6 = (f32[512,512]{1,0:T(8,128)S(1)}, f32[512,512]{1,0:T(8,128)}, u32[]{:S(2)}, u32[]{:S(2)}) collective-permute-start(f32[512,512]{1,0:T(8,128)S(1)} %copy-done), channel_id=1, source_target_pairs={{1,5}} | collective-permute-start | bytes 3145736 | tf_op jit(solution)/shard_map/ppermute | solution.py:512
  28.0 3.3 %copy-start.5 = (f32[512,512]{1,0:T(8,128)}, f32[512,512]{1,0:T(8,128)S(1)}, u32[]{:S(2)}) copy-start(f32[512,512]{1,0:T(8,128)S(1)} %collective-permute-done.refs_0_.refs_1_) | copy-start | bytes 3145732
  28.0 16.1 %collective-permute-start.16 = (f32[256,512]{1,0:T(8,128)}, f32[256,512]{1,0:T(8,128)}, u32[]{:S(2)}, u32[]{:S(2)}) collective-permute-start(f32[256,512]{1,0:T(8,128)} %get-tuple-element.14), channel_id=1, source_target_pairs={{0,1},{8,9},{12,13},{16,17},{20,21},{24,25},{28,29},{9,10},{13,14}... | collective-permute-start | bytes 1572872 | tf_op jit(solution)/shard_map/ppermute | solution.py:512
  29.3 26.0 %collective-permute-start.14 = (f32[256,512]{1,0:T(8,128)}, f32[256,512]{1,0:T(8,128)}, u32[]{:S(2)}, u32[]{:S(2)}) collective-permute-start(f32[256,512]{1,0:T(8,128)} %collective-permute-done.13.refs_4_), channel_id=1, source_target_pairs={{9,10},{13,14},{17,18},{21,22},{25,26},{29,30},{10,11},{14,15},{18... | collective-permute-start | bytes 1572872 | tf_op jit(solution)/shard_map/ppermute | solution.py:512
  31.3 36.7 %collective-permute-start.3 = (f32[512,512]{1,0:T(8,128)}, f32[512,512]{1,0:T(8,128)}, u32[]{:S(2)}, u32[]{:S(2)}) collective-permute-start(f32[512,512]{1,0:T(8,128)} %shard_map.42.refs_1_), channel_id=1, source_target_pairs={{0,8},{1,9},{2,10},{3,11}} | collective-permute-start | bytes 3145736 | tf_op jit(solution)/shard_map/ppermute | solution.py:512
  39.2 30.3 %copy-start.2 = (f32[512,512]{1,0:T(8,128)}, f32[512,512]{1,0:T(8,128)S(1)}, u32[]{:S(2)}) copy-start(f32[512,512]{1,0:T(8,128)S(1)} %broadcast_select_fusion.refs_9_.refs_13_) | copy-start | bytes 3145732
  39.2 32.0 %collective-permute-start.20 = (f32[512,512]{1,0:T(8,128)S(1)}, f32[512,512]{1,0:T(8,128)S(1)}, u32[]{:S(2)}, u32[]{:S(2)}) collective-permute-start(f32[512,512]{1,0:T(8,128)S(1)} %broadcast_select_fusion.refs_9_.refs_13_), channel_id=1, source_target_pairs={{16,20},{20,16},{24,28},{28,24},{17,21},{21,17},{25,29},{29,25},{1... | collective-permute-start | bytes 3145736 | tf_op jit(solution)/shard_map/ppermute | solution.py:512
  44.1 22.5 %collective-permute-start.17 = (f32[256,512]{1,0:T(8,128)}, f32[256,512]{1,0:T(8,128)}, u32[]{:S(2)}, u32[]{:S(2)}) collective-permute-start(f32[256,512]{1,0:T(8,128)} %collective-permute-done.16.refs_7_), channel_id=1, source_target_pairs={{9,10},{13,14},{17,18},{21,22},{25,26},{29,30},{10,11},{14,15},{18... | collective-permute-start | bytes 1572872 | tf_op jit(solution)/shard_map/ppermute | solution.py:512
  55.3 14.2 %collective-permute-start.15 = (f32[256,512]{1,0:T(8,128)}, f32[256,512]{1,0:T(8,128)}, u32[]{:S(2)}, u32[]{:S(2)}) collective-permute-start(f32[256,512]{1,0:T(8,128)} %collective-permute-done.14.refs_5_), channel_id=1, source_target_pairs={{10,11},{14,15},{18,19},{22,23},{26,27},{30,31}} | collective-permute-start | bytes 1572872 | tf_op jit(solution)/shard_map/ppermute | solution.py:512
  59.5 25.5 %collective-permute-start.7 = (f32[264,512]{1,0:T(8,128)}, f32[264,512]{1,0:T(8,128)}, u32[]{:S(2)}, u32[]{:S(2)}) collective-permute-start(f32[264,512]{1,0:T(8,128)} %shard_map.44.refs_0_), channel_id=1, source_target_pairs={{5,4}} | collective-permute-start | bytes 1622024 | tf_op jit(solution)/shard_map/ppermute | solution.py:512
  66.6 18.4 %collective-permute-start.8 = (f32[264,512]{1,0:T(8,128)}, f32[264,512]{1,0:T(8,128)}, u32[]{:S(2)}, u32[]{:S(2)}) collective-permute-start(f32[264,512]{1,0:T(8,128)} %shard_map.44.refs_0_), channel_id=1, source_target_pairs={{5,6}} | collective-permute-start | bytes 1622024 | tf_op jit(solution)/shard_map/ppermute | solution.py:512
  68.0 16.9 %collective-permute-start.9 = (f32[264,512]{1,0:T(8,128)}, f32[264,512]{1,0:T(8,128)}, u32[]{:S(2)}, u32[]{:S(2)}) collective-permute-start(f32[264,512]{1,0:T(8,128)} %shard_map.44.refs_0_), channel_id=1, source_target_pairs={{5,7}} | collective-permute-start | bytes 1622024 | tf_op jit(solution)/shard_map/ppermute | solution.py:512
  69.6 21.7 %collective-permute-start.4 = (f32[512,512]{1,0:T(8,128)}, f32[512,512]{1,0:T(8,128)}, u32[]{:S(2)}, u32[]{:S(2)}) collective-permute-start(f32[512,512]{1,0:T(8,128)} %shard_map.43), channel_id=1, source_target_pairs={{0,16},{8,24},{1,17},{9,25},{2,18},{10,26},{3,19},{11,27}} | collective-permute-start | bytes 3145736 | tf_op jit(solution)/shard_map/ppermute | solution.py:512
  83.5 2.2 %copy-start.1 = (f32[512,512]{1,0:T(8,128)S(1)}, f32[512,512]{1,0:T(8,128)}, u32[]{:S(2)}) copy-start(f32[512,512]{1,0:T(8,128)} %get-tuple-element.11.refs_1_.own_ref.refs_0_) | copy-start | bytes 3145732
  83.5 7.8 %copy-start.3 = (f32[512,512]{1,0:T(8,128)S(1)}, f32[512,512]{1,0:T(8,128)}, u32[]{:S(2)}) copy-start(f32[512,512]{1,0:T(8,128)} %shard_map.43) | copy-start | bytes 3145732
  83.5 36.9 %collective-permute-start.21 = (f32[1024,512]{1,0:T(8,128)}, f32[1024,512]{1,0:T(8,128)}, u32[]{:S(2)}, u32[]{:S(2)}) collective-permute-start(f32[1024,512]{1,0:T(8,128)} %get-tuple-element.16.refs_4_), channel_id=1, source_target_pairs={{26,30}} | collective-permute-start | bytes 6291464 | tf_op jit(solution)/shard_map/ppermute | solution.py:512
  85.0 4.0 %collective-permute-start.10 = (f32[264,512]{1,0:T(8,128)}, f32[264,512]{1,0:T(8,128)S(1)}, u32[]{:S(2)}, u32[]{:S(2)}) collective-permute-start(f32[264,512]{1,0:T(8,128)} %shard_map.45.refs_1_), channel_id=1, source_target_pairs={{4,20},{5,21},{6,22},{7,23}} | collective-permute-start | bytes 1622024 | tf_op jit(solution)/shard_map/ppermute | solution.py:512
  85.7 26.2 %collective-permute-start.23 = (f32[512,512]{1,0:T(8,128)S(1)}, f32[512,512]{1,0:T(8,128)}, u32[]{:S(2)}, u32[]{:S(2)}) collective-permute-start(f32[512,512]{1,0:T(8,128)S(1)} %copy-done.1), channel_id=1, source_target_pairs={{5,6}} | collective-permute-start | bytes 3145736 | tf_op jit(solution)/shard_map/ppermute | solution.py:512
  87.4 26.6 %collective-permute-start.24 = (f32[512,512]{1,0:T(8,128)S(1)}, f32[512,512]{1,0:T(8,128)}, u32[]{:S(2)}, u32[]{:S(2)}) collective-permute-start(f32[512,512]{1,0:T(8,128)S(1)} %copy-done.1), channel_id=1, source_target_pairs={{5,7}} | collective-permute-start | bytes 3145736 | tf_op jit(solution)/shard_map/ppermute | solution.py:512
  89.8 20.6 %copy-start.4 = (f32[264,512]{1,0:T(8,128)S(1)}, f32[264,512]{1,0:T(8,128)}, u32[]{:S(2)}) copy-start(f32[264,512]{1,0:T(8,128)} %shard_map.46) | copy-start | bytes 1622020
  89.9 20.6 %collective-permute-start.11 = (f32[264,512]{1,0:T(8,128)}, f32[264,512]{1,0:T(8,128)S(1)}, u32[]{:S(2)}, u32[]{:S(2)}) collective-permute-start(f32[264,512]{1,0:T(8,128)} %shard_map.46), channel_id=1, source_target_pairs={{4,12},{20,28},{5,13},{21,29},{6,14},{22,30},{7,15},{23,31}} | collective-permute-start | bytes 1622024 | tf_op jit(solution)/shard_map/ppermute | solution.py:512
  92.5 27.9 %collective-permute-start.5 = (f32[512,512]{1,0:T(8,128)}, f32[512,512]{1,0:T(8,128)}, u32[]{:S(2)}, u32[]{:S(2)}) collective-permute-start(f32[512,512]{1,0:T(8,128)} %broadcast_select_fusion.1.refs_2_), channel_id=1, source_target_pairs={{0,4},{8,12},{16,20},{24,28},{1,5},{9,13},{17,21},{25,29},{2,6},{1... | collective-permute-start | bytes 3145736 | tf_op jit(solution)/shard_map/ppermute | solution.py:512
  110.6 9.8 %copy-start.7 = (f32[264,512]{1,0:T(8,128)}, f32[264,512]{1,0:T(8,128)S(1)}, u32[]{:S(2)}) copy-start(f32[264,512]{1,0:T(8,128)S(1)} %broadcast_select_fusion.2.refs_3_) | copy-start | bytes 1622020
  110.6 9.8 %collective-permute-start.12 = (f32[264,512]{1,0:T(8,128)S(1)}, f32[264,512]{1,0:T(8,128)S(1)}, u32[]{:S(2)}, u32[]{:S(2)}) collective-permute-start(f32[264,512]{1,0:T(8,128)S(1)} %broadcast_select_fusion.2.refs_3_), channel_id=1, source_target_pairs={{4,0},{12,8},{20,16},{28,24},{5,1},{13,9},{21,17},{29,25},{6,2},{1... | collective-permute-start | bytes 1622024 | tf_op jit(solution)/shard_map/ppermute | solution.py:512
  111.9 8.5 %collective-permute-start.22 = (f32[256,512]{1,0:T(8,128)}, f32[256,512]{1,0:T(8,128)S(1)}, u32[]{:S(2)}, u32[]{:S(2)}) collective-permute-start(f32[256,512]{1,0:T(8,128)} %collective-permute-done.17.refs_8_), channel_id=1, source_target_pairs={{10,11},{14,15},{18,19},{22,23},{26,27},{30,31}} | collective-permute-start | bytes 1572872 | tf_op jit(solution)/shard_map/ppermute | solution.py:512
  (5 other events, 5.6 us)

commit v3 on v2

--- a/solution.py
+++ b/solution.py
@@ -285,10 +285,10 @@
     return choices + [(c == b, parts[b - 2]) for b in range(2, cols)]
 
 
-def panel_kernel(cols, cycles, tiles, *refs):
+def panel_kernel(cols, tiles, *refs):
     hops = cols - 1
-    (own, back, diag, near_held), low, high, mine, other, held, (pair_ref, near_ref), first_t, part, rest = split(
-        refs, 4, hops, hops - 1, tiles, tiles, tiles, 2, tiles, tiles, 2
+    (own, back, diag), low, high, mine, other, held, (pair_ref,), first_t, part, rest = split(
+        refs, 3, hops, hops - 1, tiles, tiles, tiles, 1, tiles, tiles, 2
     )
     dinv, sems = rest
     half = low[0].shape[0]
@@ -300,7 +300,6 @@
     waits = [
         fetch(dinv, sems.at[0], [(always, diag)]),
         fetch(pair_ref.at[top], sems.at[1], row_choices(cols, 0, half, own, low)),
-        fetch(near_ref, sems.at[2], [(always, near_held)]),
     ]
     for i, parts in enumerate((low, high)):
         choices = row_choices(cols, i, half, own, parts, back)
@@ -339,15 +338,10 @@
 
     lax.fori_loop(0, jnp.where(full, 2, 1), rows_of, 0)
 
-    @pl.when(full & (c >= 2) & (r == (cycles - 1) * cols + c))
-    def _():
-        tile = slice(0, 2 * half)
-        near_ref[...] = near_ref[...] - nt(pair_ref[tile, :], pair_ref[tile, :])
-
 
 def final_kernel(cols, cycles, tiles, *refs):
-    (corner_odd, piece_even, corner_even, piece_odd, pair, near_pair, held, near_part, last_rows, diag), arrivals, first_t, mine, other, partial, outs, rest = split(
-        refs, 10, cols // 2, tiles, tiles, tiles, tiles, 2, 8
+    (corner_odd, piece_even, corner_even, piece_odd, pair, near_pair, held, last_rows, diag), arrivals, first_t, mine, other, partial, outs, rest = split(
+        refs, 9, cols // 2, tiles, tiles, tiles, tiles, 2, 8
     )
     panels_ref, trailing_ref = outs
     packed, corner, stacks, first, second, total, near_total, sems = rest
@@ -369,15 +363,13 @@
         found = r >= (t + jnp.where(c < 2, 1, 0)) * cols + c
         return found & jnp.logical_not(own | near) if t + 1 == cycles else found
 
-    mine_late = own & late
-
     @pl.when(near)
     def _():
         pltpu.make_async_copy(near_pair, near_stack, sems.at[1]).start()
 
     @pl.when(own | near)
     def _():
-        fetch(near_total, sems.at[2], [(own & (c < cols - 1), near_part), (near | mine_late, held)])
+        pltpu.make_async_copy(held, near_total, sems.at[2]).start()
 
     @pl.when(late)
     def _():
@@ -407,10 +399,6 @@
         fetch(packed, sems.at[3], [(always, piece_odd)])()
         corner[...] = corner_odd[...]
 
-    @pl.when(near)
-    def _():
-        pltpu.make_async_copy(near_pair, near_stack, sems.at[1]).wait()
-
     @pl.when(jnp.logical_not(late))
     def _():
         pltpu.make_async_copy(pair, stack, sems.at[0]).wait()
@@ -435,6 +423,10 @@
     g_first, g_below, g_second_t = unpack(packed[...])
 
     def solve(i, carry):
+        @pl.when((i == 1) & near)
+        def _():
+            pltpu.make_async_copy(near_pair, near_stack, sems.at[1]).wait()
+
         @pl.when((i == 0) | near)
         def _():
             target = stacks.at[i]
@@ -459,7 +451,10 @@
             rows, start = (top, b * width) if 2 * b < cols else (bottom, b * width - tile)
             panels_ref[...] = stack[rows, start : start + width]
 
-    trailing_ref[...] = jnp.zeros_like(trailing_ref)
+    @pl.when(jnp.logical_not(own | near))
+    def _():
+        trailing_ref[...] = jnp.zeros_like(trailing_ref)
+
     for wait in waits:
         wait()
 
@@ -488,9 +483,6 @@
     @pl.when(own | near)
     def _():
         pltpu.make_async_copy(held, near_total, sems.at[2]).wait()
-
-    @pl.when(near | (own & late))
-    def _():
         near_total[...] = near_total[...] - nt(stack[top, :], stacks[which, top])
 
     @pl.when(own | near)
@@ -647,11 +639,11 @@
     piece_even = trade(piece_odd, everyone, (1,))
 
     product = 2 * tile**3
-    pair, near_part, *products = call(
-        functools.partial(panel_kernel, cols, cycles, tiles),
-        [(2 * tile, tile), whole] + [whole] * (2 * tiles),
+    pair, *products = call(
+        functools.partial(panel_kernel, cols, tiles),
+        [(2 * tile, tile)] + [whole] * (2 * tiles),
         [
-            lead, back, diag_inverse, held[-1],
+            lead, back, diag_inverse,
             *moved[0], *moved[1][:-1], *mine, *other, *held[:tiles],
         ],
         [vmem(*whole), copies(6 + 2 * tiles)],
@@ -665,7 +657,7 @@
         functools.partial(final_kernel, cols, cycles, tiles),
         [(tile, 2 * tile // cols), covariance.shape],
         [
-            corner_odd, piece_even, corner, piece_odd, pair, near_pair, held[-1], near_part,
+            corner_odd, piece_even, corner, piece_odd, pair, near_pair, held[-1],
             moved[1][-1], diag_inverse, *passed,
             *first_t, *mine, *other, *partial,
         ],

time: 141 us -> 141 us (level)
    unnamed x24 -> x28, local copies, waits for them, and re-layouts: 2.88 us -> 3.84 us
  transfers between devices with their start and end apart: 25 -> 25, of which waited for: 7 -> 6; matrix products, arithmetic and copies ran while one was open for 2% -> 2% of each run, Pallas kernels for 10% -> 9%
where the time goes in v3:
time: 141 us; the launch traced here: 140 us
  waiting for transfers between devices  56.1 us (40%)
  starting transfers between devices  40.6 us (29%)
  Pallas kernels  35.8 us (25%)
  local copies, waits for them, and re-layouts  3.84 us (3%)
  other arithmetic  2.71 us (2%)
    ppermute x25, waiting for transfers between devices, send(): return lax.ppermute(value, AXES, flat)  56.1 us
    ppermute x25, starting transfers between devices, send(): return lax.ppermute(value, AXES, flat)  40.6 us
    pallas_call x4, Pallas kernels, call(): pl.pallas_call(kernel, out_shape=outs, in_specs=[pl.BlockSpec(memory_spac...  35.7 us
    unnamed x28, local copies, waits for them, and re-layouts  3.84 us
  transfers between devices with their start and end apart: 25, of which 6 were waited for; matrix products, arithmetic and copies ran while one was open for 2% of the time, Pallas kernels for 9%

profile of v3, /device:TPU:23, one launch (start us, length us, event | category | flops | bytes accessed | tf_op | source)
XLA Modules:
  0.0 140.3 jit_solution(1754177236335423216)
XLA Ops:
  0.6 4.3 %shard_map.41 = (f32[512,512]{1,0:T(8,128)}, f32[256,512]{1,0:T(8,128)}, f32[256,512]{1,0:T(8,128)}, f32[512,512]{1,0:T(8,128)}, f32[512,512]{1,0:T(8,128)}) custom-call(f32[512,2,512]{2,1,0:T(2,128)} %cov_ref.1, f32[512,512]{1,0:T(8,128)} %refs_8_.1), custom_call_target="tpu_custom_call" | custom-call | bytes 7340032 | tf_op jit(solution)/shard_map/pallas_call | solution.py:137
  6.6 1.6 %collective-permute-start.1 = (f32[512,512]{1,0:T(8,128)}, f32[512,512]{1,0:T(8,128)}, u32[]{:S(2)}, u32[]{:S(2)}) collective-permute-start(f32[512,512]{1,0:T(8,128)} %get-tuple-element.10.refs_1_.own_ref.refs_0_), channel_id=1, source_target_pairs={{1,2}} | collective-permute-start | bytes 3145736 | tf_op jit(solution)/shard_map/ppermute | solution.py:504
  8.2 1.7 %collective-permute-start.2 = (f32[512,512]{1,0:T(8,128)}, f32[512,512]{1,0:T(8,128)}, u32[]{:S(2)}, u32[]{:S(2)}) collective-permute-start(f32[512,512]{1,0:T(8,128)} %get-tuple-element.10.refs_1_.own_ref.refs_0_), channel_id=1, source_target_pairs={{1,3}} | collective-permute-start | bytes 3145736 | tf_op jit(solution)/shard_map/ppermute | solution.py:504
  10.9 1.3 collective-permute-start.19
  12.2 1.3 collective-permute-start.13
  13.5 13.7 %collective-permute-done.13.refs_3_ = f32[256,512]{1,0:T(8,128)S(1)} collective-permute-done((f32[256,512]{1,0:T(8,128)}, f32[256,512]{1,0:T(8,128)S(1)}, u32[]{:S(2)}, u32[]{:S(2)}) %collective-permute-start.13) | collective-permute-done | bytes 524320 | tf_op jit(solution)/shard_map/ppermute | solution.py:504
  27.2 1.6 %collective-permute-start.6 = (f32[512,512]{1,0:T(8,128)S(1)}, f32[512,512]{1,0:T(8,128)}, u32[]{:S(2)}, u32[]{:S(2)}) collective-permute-start(f32[512,512]{1,0:T(8,128)S(1)} %copy-done), channel_id=1, source_target_pairs={{1,5}} | collective-permute-start | bytes 3145736 | tf_op jit(solution)/shard_map/ppermute | solution.py:504
  28.9 1.4 %collective-permute-start.16 = (f32[256,512]{1,0:T(8,128)}, f32[256,512]{1,0:T(8,128)}, u32[]{:S(2)}, u32[]{:S(2)}) collective-permute-start(f32[256,512]{1,0:T(8,128)} %get-tuple-element.12), channel_id=1, source_target_pairs={{0,1},{8,9},{12,13},{16,17},{20,21},{24,25},{28,29},{9,10},{13,14}... | collective-permute-start | bytes 1572872 | tf_op jit(solution)/shard_map/ppermute | solution.py:504
  30.3 1.9 %collective-permute-start.14 = (f32[256,512]{1,0:T(8,128)}, f32[256,512]{1,0:T(8,128)}, u32[]{:S(2)}, u32[]{:S(2)}) collective-permute-start(f32[256,512]{1,0:T(8,128)} %copy-done.12), channel_id=1, source_target_pairs={{9,10},{13,14},{17,18},{21,22},{25,26},{29,30},{10,11},{14,15},{18... | collective-permute-start | bytes 1572872 | tf_op jit(solution)/shard_map/ppermute | solution.py:504
  32.3 1.7 %collective-permute-start.3 = (f32[512,512]{1,0:T(8,128)}, f32[512,512]{1,0:T(8,128)}, u32[]{:S(2)}, u32[]{:S(2)}) collective-permute-start(f32[512,512]{1,0:T(8,128)} %shard_map.42.refs_1_), channel_id=1, source_target_pairs={{0,8},{1,9},{2,10},{3,11}} | collective-permute-start | bytes 3145736 | tf_op jit(solution)/shard_map/ppermute | solution.py:504
  34.0 4.7 %collective-permute-done.19 = f32[512,512]{1,0:T(8,128)} collective-permute-done((f32[512,512]{1,0:T(8,128)}, f32[512,512]{1,0:T(8,128)}, u32[]{:S(2)}, u32[]{:S(2)}) %collective-permute-start.19) | collective-permute-done | bytes 1048608 | tf_op jit(solution)/shard_map/ppermute | solution.py:504
  38.7 1.4 %broadcast_select_fusion.refs_8_.refs_12_ = f32[512,512]{1,0:T(8,128)S(1)} fusion(f32[512,512]{1,0:T(8,128)} %collective-permute-done.19, f32[512,512]{1,0:T(8,128)S(1)} %copy-done.7, pred[]{:T(512)S(6)} %select_n.53), kind=kLoop, calls=%fused_computation | loop fusion | flops 262144 | bytes 3145729 | tf_op jit(solution)/shard_map/jit(_where)/select_n | solution.py:562
  40.1 4.0 %collective-permute-start.20 = (f32[512,512]{1,0:T(8,128)S(1)}, f32[512,512]{1,0:T(8,128)S(1)}, u32[]{:S(2)}, u32[]{:S(2)}) collective-permute-start(f32[512,512]{1,0:T(8,128)S(1)} %broadcast_select_fusion.refs_8_.refs_12_), channel_id=1, source_target_pairs={{16,20},{20,16},{24,28},{28,24},{17,21},{21,17},{25,29},{29,25},{1... | collective-permute-start | bytes 3145736 | tf_op jit(solution)/shard_map/ppermute | solution.py:504
  44.1 3.2 %collective-permute-start.17 = (f32[256,512]{1,0:T(8,128)}, f32[256,512]{1,0:T(8,128)}, u32[]{:S(2)}, u32[]{:S(2)}) collective-permute-start(f32[256,512]{1,0:T(8,128)} %collective-permute-done.16.refs_6_), channel_id=1, source_target_pairs={{9,10},{13,14},{17,18},{21,22},{25,26},{29,30},{10,11},{14,15},{18... | collective-permute-start | bytes 1572872 | tf_op jit(solution)/shard_map/ppermute | solution.py:504
  47.3 7.1 %collective-permute-done.14.refs_4_ = f32[256,512]{1,0:T(8,128)} collective-permute-done((f32[256,512]{1,0:T(8,128)}, f32[256,512]{1,0:T(8,128)}, u32[]{:S(2)}, u32[]{:S(2)}) %collective-permute-start.14) | collective-permute-done | bytes 524320 | tf_op jit(solution)/shard_map/ppermute | solution.py:504
  54.4 2.1 %collective-permute-start.15 = (f32[256,512]{1,0:T(8,128)}, f32[256,512]{1,0:T(8,128)}, u32[]{:S(2)}, u32[]{:S(2)}) collective-permute-start(f32[256,512]{1,0:T(8,128)} %collective-permute-done.14.refs_4_), channel_id=1, source_target_pairs={{10,11},{14,15},{18,19},{22,23},{26,27},{30,31}} | collective-permute-start | bytes 1572872 | tf_op jit(solution)/shard_map/ppermute | solution.py:504
  56.5 2.1 %shard_map.44.refs_0_ = f32[264,512]{1,0:T(8,128)} custom-call(f32[512,512]{1,0:T(8,128)} %collective-permute-done.6.corner_ref, f32[512,512]{1,0:T(8,128)} %get-tuple-element.10.refs_1_.own_ref.refs_0_), custom_call_target="tpu_custom_call" | custom-call | bytes 2637824 | tf_op jit(solution)/shard_map/pallas_call | solution.py:137
  58.6 1.7 %collective-permute-start.7 = (f32[264,512]{1,0:T(8,128)}, f32[264,512]{1,0:T(8,128)}, u32[]{:S(2)}, u32[]{:S(2)}) collective-permute-start(f32[264,512]{1,0:T(8,128)} %shard_map.44.refs_0_), channel_id=1, source_target_pairs={{5,4}} | collective-permute-start | bytes 1622024 | tf_op jit(solution)/shard_map/ppermute | solution.py:504
  60.2 5.4 %collective-permute-done.17.refs_7_ = f32[256,512]{1,0:T(8,128)} collective-permute-done((f32[256,512]{1,0:T(8,128)}, f32[256,512]{1,0:T(8,128)}, u32[]{:S(2)}, u32[]{:S(2)}) %collective-permute-start.17) | collective-permute-done | bytes 524320 | tf_op jit(solution)/shard_map/ppermute | solution.py:504
  65.6 1.5 %collective-permute-start.8 = (f32[264,512]{1,0:T(8,128)}, f32[264,512]{1,0:T(8,128)}, u32[]{:S(2)}, u32[]{:S(2)}) collective-permute-start(f32[264,512]{1,0:T(8,128)} %shard_map.44.refs_0_), channel_id=1, source_target_pairs={{5,6}} | collective-permute-start | bytes 1622024 | tf_op jit(solution)/shard_map/ppermute | solution.py:504
  67.1 1.5 %collective-permute-start.9 = (f32[264,512]{1,0:T(8,128)}, f32[264,512]{1,0:T(8,128)}, u32[]{:S(2)}, u32[]{:S(2)}) collective-permute-start(f32[264,512]{1,0:T(8,128)} %shard_map.44.refs_0_), channel_id=1, source_target_pairs={{5,7}} | collective-permute-start | bytes 1622024 | tf_op jit(solution)/shard_map/ppermute | solution.py:504
  68.6 1.6 %collective-permute-start.4 = (f32[512,512]{1,0:T(8,128)}, f32[512,512]{1,0:T(8,128)}, u32[]{:S(2)}, u32[]{:S(2)}) collective-permute-start(f32[512,512]{1,0:T(8,128)} %shard_map.43), channel_id=1, source_target_pairs={{0,16},{8,24},{1,17},{9,25},{2,18},{10,26},{3,19},{11,27}} | collective-permute-start | bytes 3145736 | tf_op jit(solution)/shard_map/ppermute | solution.py:504
  71.3 10.5 %shard_map.48 = (f32[1024,512]{1,0:T(8,128)}, f32[512,512]{1,0:T(8,128)}, f32[512,512]{1,0:T(8,128)}) custom-call(f32[512,512]{1,0:T(8,128)} %get-tuple-element.10.refs_1_.own_ref.refs_0_, f32[512,512]{1,0:T(8,128)} %copy-done.5, f32[512,512]{1,0:T(8,128)} %refs_8_.1, f32[256,512]{1,0:T(8,128)} %copy-done.12, f32[256,512]{1,0:T(8,128)} %collective-permute-done.14.refs_4_, ...), custom_call_target="tpu_custom_call" | custom-call | flops 805306368 | bytes 13107200 | tf_op jit(solution)/shard_map/pallas_call | solution.py:137
  81.9 1.4 %collective-permute-start.21 = (f32[1024,512]{1,0:T(8,128)}, f32[1024,512]{1,0:T(8,128)}, u32[]{:S(2)}, u32[]{:S(2)}) collective-permute-start(f32[1024,512]{1,0:T(8,128)} %get-tuple-element.14.refs_4_), channel_id=1, source_target_pairs={{26,30}} | collective-permute-start | bytes 6291464 | tf_op jit(solution)/shard_map/ppermute | solution.py:504
  84.1 1.6 %collective-permute-start.23 = (f32[512,512]{1,0:T(8,128)S(1)}, f32[512,512]{1,0:T(8,128)}, u32[]{:S(2)}, u32[]{:S(2)}) collective-permute-start(f32[512,512]{1,0:T(8,128)S(1)} %copy-done.1), channel_id=1, source_target_pairs={{5,6}} | collective-permute-start | bytes 3145736 | tf_op jit(solution)/shard_map/ppermute | solution.py:504
  85.8 1.7 %collective-permute-start.24 = (f32[512,512]{1,0:T(8,128)S(1)}, f32[512,512]{1,0:T(8,128)}, u32[]{:S(2)}, u32[]{:S(2)}) collective-permute-start(f32[512,512]{1,0:T(8,128)S(1)} %copy-done.1), channel_id=1, source_target_pairs={{5,7}} | collective-permute-start | bytes 3145736 | tf_op jit(solution)/shard_map/ppermute | solution.py:504
  88.3 1.4 %collective-permute-start.11 = (f32[264,512]{1,0:T(8,128)}, f32[264,512]{1,0:T(8,128)S(1)}, u32[]{:S(2)}, u32[]{:S(2)}) collective-permute-start(f32[264,512]{1,0:T(8,128)} %shard_map.46), channel_id=1, source_target_pairs={{4,12},{20,28},{5,13},{21,29},{6,14},{22,30},{7,15},{23,31}} | collective-permute-start | bytes 1622024 | tf_op jit(solution)/shard_map/ppermute | solution.py:504
  92.2 18.8 %collective-permute-done.11 = f32[264,512]{1,0:T(8,128)S(1)} collective-permute-done((f32[264,512]{1,0:T(8,128)}, f32[264,512]{1,0:T(8,128)S(1)}, u32[]{:S(2)}, u32[]{:S(2)}) %collective-permute-start.11) | collective-permute-done | bytes 540704 | tf_op jit(solution)/shard_map/ppermute | solution.py:504
  111.1 1.3 collective-permute-start.12
  112.5 1.5 %collective-permute-start.22 = (f32[256,512]{1,0:T(8,128)}, f32[256,512]{1,0:T(8,128)S(1)}, u32[]{:S(2)}, u32[]{:S(2)}) collective-permute-start(f32[256,512]{1,0:T(8,128)} %collective-permute-done.17.refs_7_), channel_id=1, source_target_pairs={{10,11},{14,15},{18,19},{22,23},{26,27},{30,31}} | collective-permute-start | bytes 1572872 | tf_op jit(solution)/shard_map/ppermute | solution.py:504
  114.0 6.4 %collective-permute-done.22.refs_7_ = f32[256,512]{1,0:T(8,128)S(1)} collective-permute-done((f32[256,512]{1,0:T(8,128)}, f32[256,512]{1,0:T(8,128)S(1)}, u32[]{:S(2)}, u32[]{:S(2)}) %collective-permute-start.22) | collective-permute-done | bytes 524320 | tf_op jit(solution)/shard_map/ppermute | solution.py:504
  121.4 18.8 %shard_map.49 = (f32[512,256]{1,0:T(8,128)}, f32[512,2,512]{2,1,0:T(2,128)}) custom-call(f32[512,512]{1,0:T(8,128)} %collective-permute-done.5.refs_0_, f32[264,512]{1,0:T(8,128)} %copy-done.11, f32[512,512]{1,0:T(8,128)} %broadcast_select_fusion.1.refs_2_, f32[264,512]{1,0:T(8,128)} %copy-done.8, f32[1024,512]{1,0:T(8,128)} %get-tuple-element.14.refs_4_, ...), custom_call_target="tpu_custom_call" | custom-call | flops 1342177280 | bytes 18907136 | tf_op jit(solution)/shard_map/pallas_call | solution.py:137
  (58 shorter events, 8.9 us)
Async XLA Ops:
  4.9 22.3 %copy-start = (f32[512,512]{1,0:T(8,128)S(1)}, f32[512,512]{1,0:T(8,128)}, u32[]{:S(2)}) copy-start(f32[512,512]{1,0:T(8,128)} %get-tuple-element.10.refs_1_.own_ref.refs_0_) | copy-start | bytes 3145732
  5.0 4.9 %collective-permute-start.18 = (f32[512,512]{1,0:T(8,128)}, f32[512,512]{1,0:T(8,128)S(1)}, u32[]{:S(2)}, u32[]{:S(2)}) collective-permute-start(f32[512,512]{1,0:T(8,128)} %get-tuple-element.13.refs_1_.refs_10_), channel_id=1, source_target_pairs={{0,8},{1,9},{2,10},{3,11},{4,20},{5,21},{6,22},{7,23}} | collective-permute-start | bytes 3145736 | tf_op jit(solution)/shard_map/ppermute | solution.py:504
  5.8 23.0 %collective-permute-start = (f32[512,512]{1,0:T(8,128)}, f32[512,512]{1,0:T(8,128)S(1)}, u32[]{:S(2)}, u32[]{:S(2)}) collective-permute-start(f32[512,512]{1,0:T(8,128)} %get-tuple-element.10.refs_1_.own_ref.refs_0_), channel_id=1, source_target_pairs={{1,0},{17,16},{21,20},{25,24},{29,28}} | collective-permute-start | bytes 3145736 | tf_op jit(solution)/shard_map/ppermute | solution.py:504
  6.6 23.7 %collective-permute-start.1 = (f32[512,512]{1,0:T(8,128)}, f32[512,512]{1,0:T(8,128)}, u32[]{:S(2)}, u32[]{:S(2)}) collective-permute-start(f32[512,512]{1,0:T(8,128)} %get-tuple-element.10.refs_1_.own_ref.refs_0_), channel_id=1, source_target_pairs={{1,2}} | collective-permute-start | bytes 3145736 | tf_op jit(solution)/shard_map/ppermute | solution.py:504
  8.2 24.0 %collective-permute-start.2 = (f32[512,512]{1,0:T(8,128)}, f32[512,512]{1,0:T(8,128)}, u32[]{:S(2)}, u32[]{:S(2)}) collective-permute-start(f32[512,512]{1,0:T(8,128)} %get-tuple-element.10.refs_1_.own_ref.refs_0_), channel_id=1, source_target_pairs={{1,3}} | collective-permute-start | bytes 3145736 | tf_op jit(solution)/shard_map/ppermute | solution.py:504
  10.9 27.8 %collective-permute-start.19 = (f32[512,512]{1,0:T(8,128)}, f32[512,512]{1,0:T(8,128)}, u32[]{:S(2)}, u32[]{:S(2)}) collective-permute-start(f32[512,512]{1,0:T(8,128)} %shard_map.47), channel_id=1, source_target_pairs={{0,16},{8,24},{1,17},{9,25},{2,18},{10,26},{3,19},{11,27},{20,28},... | collective-permute-start | bytes 3145736 | tf_op jit(solution)/shard_map/ppermute | solution.py:504
  12.2 15.0 %collective-permute-start.13 = (f32[256,512]{1,0:T(8,128)}, f32[256,512]{1,0:T(8,128)S(1)}, u32[]{:S(2)}, u32[]{:S(2)}) collective-permute-start(f32[256,512]{1,0:T(8,128)} %get-tuple-element.11), channel_id=1, source_target_pairs={{0,1},{8,9},{12,13},{16,17},{20,21},{24,25},{28,29},{9,10},{13,14}... | collective-permute-start | bytes 1572872 | tf_op jit(solution)/shard_map/ppermute | solution.py:504
  27.2 29.3 %collective-permute-start.6 = (f32[512,512]{1,0:T(8,128)S(1)}, f32[512,512]{1,0:T(8,128)}, u32[]{:S(2)}, u32[]{:S(2)}) collective-permute-start(f32[512,512]{1,0:T(8,128)S(1)} %copy-done), channel_id=1, source_target_pairs={{1,5}} | collective-permute-start | bytes 3145736 | tf_op jit(solution)/shard_map/ppermute | solution.py:504
  28.9 3.4 %copy-start.5 = (f32[512,512]{1,0:T(8,128)}, f32[512,512]{1,0:T(8,128)S(1)}, u32[]{:S(2)}) copy-start(f32[512,512]{1,0:T(8,128)S(1)} %collective-permute-done.refs_0_.refs_1_) | copy-start | bytes 3145732
  28.9 9.8 %copy-start.7 = (f32[512,512]{1,0:T(8,128)S(1)}, f32[512,512]{1,0:T(8,128)}, u32[]{:S(2)}) copy-start(f32[512,512]{1,0:T(8,128)} %shard_map.47) | copy-start | bytes 3145732
  28.9 15.2 %collective-permute-start.16 = (f32[256,512]{1,0:T(8,128)}, f32[256,512]{1,0:T(8,128)}, u32[]{:S(2)}, u32[]{:S(2)}) collective-permute-start(f32[256,512]{1,0:T(8,128)} %get-tuple-element.12), channel_id=1, source_target_pairs={{0,1},{8,9},{12,13},{16,17},{20,21},{24,25},{28,29},{9,10},{13,14}... | collective-permute-start | bytes 1572872 | tf_op jit(solution)/shard_map/ppermute | solution.py:504
  30.3 24.1 %collective-permute-start.14 = (f32[256,512]{1,0:T(8,128)}, f32[256,512]{1,0:T(8,128)}, u32[]{:S(2)}, u32[]{:S(2)}) collective-permute-start(f32[256,512]{1,0:T(8,128)} %copy-done.12), channel_id=1, source_target_pairs={{9,10},{13,14},{17,18},{21,22},{25,26},{29,30},{10,11},{14,15},{18... | collective-permute-start | bytes 1572872 | tf_op jit(solution)/shard_map/ppermute | solution.py:504
  32.3 34.8 %collective-permute-start.3 = (f32[512,512]{1,0:T(8,128)}, f32[512,512]{1,0:T(8,128)}, u32[]{:S(2)}, u32[]{:S(2)}) collective-permute-start(f32[512,512]{1,0:T(8,128)} %shard_map.42.refs_1_), channel_id=1, source_target_pairs={{0,8},{1,9},{2,10},{3,11}} | collective-permute-start | bytes 3145736 | tf_op jit(solution)/shard_map/ppermute | solution.py:504
  40.1 28.5 %copy-start.2 = (f32[512,512]{1,0:T(8,128)}, f32[512,512]{1,0:T(8,128)S(1)}, u32[]{:S(2)}) copy-start(f32[512,512]{1,0:T(8,128)S(1)} %broadcast_select_fusion.refs_8_.refs_12_) | copy-start | bytes 3145732
  40.1 30.1 %collective-permute-start.20 = (f32[512,512]{1,0:T(8,128)S(1)}, f32[512,512]{1,0:T(8,128)S(1)}, u32[]{:S(2)}, u32[]{:S(2)}) collective-permute-start(f32[512,512]{1,0:T(8,128)S(1)} %broadcast_select_fusion.refs_8_.refs_12_), channel_id=1, source_target_pairs={{16,20},{20,16},{24,28},{28,24},{17,21},{21,17},{25,29},{29,25},{1... | collective-permute-start | bytes 3145736 | tf_op jit(solution)/shard_map/ppermute | solution.py:504
  44.1 21.5 %collective-permute-start.17 = (f32[256,512]{1,0:T(8,128)}, f32[256,512]{1,0:T(8,128)}, u32[]{:S(2)}, u32[]{:S(2)}) collective-permute-start(f32[256,512]{1,0:T(8,128)} %collective-permute-done.16.refs_6_), channel_id=1, source_target_pairs={{9,10},{13,14},{17,18},{21,22},{25,26},{29,30},{10,11},{14,15},{18... | collective-permute-start | bytes 1572872 | tf_op jit(solution)/shard_map/ppermute | solution.py:504
  54.4 14.2 %collective-permute-start.15 = (f32[256,512]{1,0:T(8,128)}, f32[256,512]{1,0:T(8,128)}, u32[]{:S(2)}, u32[]{:S(2)}) collective-permute-start(f32[256,512]{1,0:T(8,128)} %collective-permute-done.14.refs_4_), channel_id=1, source_target_pairs={{10,11},{14,15},{18,19},{22,23},{26,27},{30,31}} | collective-permute-start | bytes 1572872 | tf_op jit(solution)/shard_map/ppermute | solution.py:504
  58.6 24.8 %collective-permute-start.7 = (f32[264,512]{1,0:T(8,128)}, f32[264,512]{1,0:T(8,128)}, u32[]{:S(2)}, u32[]{:S(2)}) collective-permute-start(f32[264,512]{1,0:T(8,128)} %shard_map.44.refs_0_), channel_id=1, source_target_pairs={{5,4}} | collective-permute-start | bytes 1622024 | tf_op jit(solution)/shard_map/ppermute | solution.py:504
  65.6 17.7 %collective-permute-start.8 = (f32[264,512]{1,0:T(8,128)}, f32[264,512]{1,0:T(8,128)}, u32[]{:S(2)}, u32[]{:S(2)}) collective-permute-start(f32[264,512]{1,0:T(8,128)} %shard_map.44.refs_0_), channel_id=1, source_target_pairs={{5,6}} | collective-permute-start | bytes 1622024 | tf_op jit(solution)/shard_map/ppermute | solution.py:504
  67.1 16.3 %collective-permute-start.9 = (f32[264,512]{1,0:T(8,128)}, f32[264,512]{1,0:T(8,128)}, u32[]{:S(2)}, u32[]{:S(2)}) collective-permute-start(f32[264,512]{1,0:T(8,128)} %shard_map.44.refs_0_), channel_id=1, source_target_pairs={{5,7}} | collective-permute-start | bytes 1622024 | tf_op jit(solution)/shard_map/ppermute | solution.py:504
  68.6 21.1 %collective-permute-start.4 = (f32[512,512]{1,0:T(8,128)}, f32[512,512]{1,0:T(8,128)}, u32[]{:S(2)}, u32[]{:S(2)}) collective-permute-start(f32[512,512]{1,0:T(8,128)} %shard_map.43), channel_id=1, source_target_pairs={{0,16},{8,24},{1,17},{9,25},{2,18},{10,26},{3,19},{11,27}} | collective-permute-start | bytes 3145736 | tf_op jit(solution)/shard_map/ppermute | solution.py:504
  81.9 7.8 %copy-start.3 = (f32[512,512]{1,0:T(8,128)S(1)}, f32[512,512]{1,0:T(8,128)}, u32[]{:S(2)}) copy-start(f32[512,512]{1,0:T(8,128)} %shard_map.43) | copy-start | bytes 3145732
  81.9 38.5 %collective-permute-start.21 = (f32[1024,512]{1,0:T(8,128)}, f32[1024,512]{1,0:T(8,128)}, u32[]{:S(2)}, u32[]{:S(2)}) collective-permute-start(f32[1024,512]{1,0:T(8,128)} %get-tuple-element.14.refs_4_), channel_id=1, source_target_pairs={{26,30}} | collective-permute-start | bytes 6291464 | tf_op jit(solution)/shard_map/ppermute | solution.py:504
  83.4 4.0 %collective-permute-start.10 = (f32[264,512]{1,0:T(8,128)}, f32[264,512]{1,0:T(8,128)S(1)}, u32[]{:S(2)}, u32[]{:S(2)}) collective-permute-start(f32[264,512]{1,0:T(8,128)} %shard_map.45.refs_1_), channel_id=1, source_target_pairs={{4,20},{5,21},{6,22},{7,23}} | collective-permute-start | bytes 1622024 | tf_op jit(solution)/shard_map/ppermute | solution.py:504
  84.1 28.3 %collective-permute-start.23 = (f32[512,512]{1,0:T(8,128)S(1)}, f32[512,512]{1,0:T(8,128)}, u32[]{:S(2)}, u32[]{:S(2)}) collective-permute-start(f32[512,512]{1,0:T(8,128)S(1)} %copy-done.1), channel_id=1, source_target_pairs={{5,6}} | collective-permute-start | bytes 3145736 | tf_op jit(solution)/shard_map/ppermute | solution.py:504
  85.8 28.3 %collective-permute-start.24 = (f32[512,512]{1,0:T(8,128)S(1)}, f32[512,512]{1,0:T(8,128)}, u32[]{:S(2)}, u32[]{:S(2)}) collective-permute-start(f32[512,512]{1,0:T(8,128)S(1)} %copy-done.1), channel_id=1, source_target_pairs={{5,7}} | collective-permute-start | bytes 3145736 | tf_op jit(solution)/shard_map/ppermute | solution.py:504
  88.3 22.8 %copy-start.4 = (f32[264,512]{1,0:T(8,128)S(1)}, f32[264,512]{1,0:T(8,128)}, u32[]{:S(2)}) copy-start(f32[264,512]{1,0:T(8,128)} %shard_map.46) | copy-start | bytes 1622020
  88.3 22.8 %collective-permute-start.11 = (f32[264,512]{1,0:T(8,128)}, f32[264,512]{1,0:T(8,128)S(1)}, u32[]{:S(2)}, u32[]{:S(2)}) collective-permute-start(f32[264,512]{1,0:T(8,128)} %shard_map.46), channel_id=1, source_target_pairs={{4,12},{20,28},{5,13},{21,29},{6,14},{22,30},{7,15},{23,31}} | collective-permute-start | bytes 1622024 | tf_op jit(solution)/shard_map/ppermute | solution.py:504
  90.9 29.5 %collective-permute-start.5 = (f32[512,512]{1,0:T(8,128)}, f32[512,512]{1,0:T(8,128)}, u32[]{:S(2)}, u32[]{:S(2)}) collective-permute-start(f32[512,512]{1,0:T(8,128)} %broadcast_select_fusion.1.refs_2_), channel_id=1, source_target_pairs={{0,4},{8,12},{16,20},{24,28},{1,5},{9,13},{17,21},{25,29},{2,6},{1... | collective-permute-start | bytes 3145736 | tf_op jit(solution)/shard_map/ppermute | solution.py:504
  111.1 9.3 %copy-start.8 = (f32[264,512]{1,0:T(8,128)}, f32[264,512]{1,0:T(8,128)S(1)}, u32[]{:S(2)}) copy-start(f32[264,512]{1,0:T(8,128)S(1)} %broadcast_select_fusion.2.refs_3_) | copy-start | bytes 1622020
  111.1 9.3 %collective-permute-start.12 = (f32[264,512]{1,0:T(8,128)S(1)}, f32[264,512]{1,0:T(8,128)S(1)}, u32[]{:S(2)}, u32[]{:S(2)}) collective-permute-start(f32[264,512]{1,0:T(8,128)S(1)} %broadcast_select_fusion.2.refs_3_), channel_id=1, source_target_pairs={{4,0},{12,8},{20,16},{28,24},{5,1},{13,9},{21,17},{29,25},{6,2},{1... | collective-permute-start | bytes 1622024 | tf_op jit(solution)/shard_map/ppermute | solution.py:504
  112.5 7.9 %collective-permute-start.22 = (f32[256,512]{1,0:T(8,128)}, f32[256,512]{1,0:T(8,128)S(1)}, u32[]{:S(2)}, u32[]{:S(2)}) collective-permute-start(f32[256,512]{1,0:T(8,128)} %collective-permute-done.17.refs_7_), channel_id=1, source_target_pairs={{10,11},{14,15},{18,19},{22,23},{26,27},{30,31}} | collective-permute-start | bytes 1572872 | tf_op jit(solution)/shard_map/ppermute | solution.py:504
  (7 other events, 8.5 us)
